TPU v7x, 768 devices: a whole 4x8x12 slice. The times are simulated.
768 devices in a mesh: energy: 96 (over x, z, y_hi), atom: 8 (over y_lo, core).
Axes of the slice: x: 4, y: 8 (y_hi: 2, y_lo: 4; y = y_hi * 4 + y_lo), z: 12, core: 2. Of those that a mesh axis runs over, the one named last changes fastest.
Arguments:
- greens: bfloat16 [2, 768, 128, 256], P(None, ('energy', 'atom')), may hold values from -6 to 6
- coupling: bfloat16 [128, 8, 256], P('atom'), may hold values from -1.5 to 1.5
- neighbours: int32 [128, 8], P('atom'), may hold values from 0 to 127, as said below
- counts: int32 [128], P('atom'), may hold values from 4 to 8, as said below
- phonon_weights: float32 [2, 16], replicated, may hold values from 0.02 to 0.12
- offsets: int32 [16], replicated, may hold values from 1 to 8, as said below
Outputs:
- self_energy: bfloat16 [2, 768, 128, 256], P(None, 'energy', 'atom')
- phonon_self: float32 [128, 128], P('atom')
- current: float32 [768, 256], P(('energy', 'atom'))
Inputs may be any that keep to these rules, and one draw needn't show every extreme that they name: `neighbours`: every entry of row a differs from a by 1 to 8; in every draw some entry lies exactly 8 from its atom. Atom a uses its first counts[a] listed neighbours; every draw holds an atom with 8 and one with 4. `offsets`: every draw holds a shift of 1 and a shift of 8.
All inputs are finite; a program needn't handle non-finite values.
Results may differ from a plain program's by a relative error of at most 0.0067.
Values may be sent and summed in bfloat16 or wider, within the bound.
No kernel may reach another device: no remote copies, remote signals or barrier semaphores. Data moves between devices by JAX's collectives and lax.ppermute only.
A program may use at most 32 MiB of HBM per device.

v0:
```python
import math

import jax
import jax.numpy as jnp
from jax import lax
from jax.sharding import PartitionSpec as P

NO = 16
NB = 8
NW = 16
REACH = 8


def with_halo(array, sides, width):
    for axis, dim in sides:
        size, length = (lax.axis_size(axis), array.shape[dim])
        up = [(i, (i + 1) % size) for i in range(size - 1)]
        down = [(j, i) for i, j in up]
        last = lax.slice_in_dim(array, length - width, length, axis=dim)
        leading = lax.slice_in_dim(array, 0, width, axis=dim)
        before = lax.ppermute(last, axis, up)
        after = lax.ppermute(leading, axis, down)
        array = jnp.concatenate([before, array, after], axis=dim)
    return array


def shift_tables(phonon_weights, offsets, energies, framed_rows):
    target = lax.broadcasted_iota(jnp.int32, (energies, framed_rows), 1)
    anchor = lax.broadcasted_iota(jnp.int32, (energies, framed_rows), 0)
    distance = (target - anchor - REACH)[None, :, :]
    shifts = offsets[:, None, None]
    upward = (distance == shifts).astype(jnp.float32)
    downward = (distance == -shifts).astype(jnp.float32)
    emission = phonon_weights[0][:, None, None]
    absorption = phonon_weights[1][:, None, None]
    table_less = jnp.sum(emission * upward + absorption * downward, axis=0)
    table_greater = jnp.sum(emission * downward + absorption * upward, axis=0)
    return (table_less.astype(jnp.bfloat16), table_greater.astype(jnp.bfloat16), upward)


def collision(sigma, green):
    energies = sigma.shape[1]
    atom_count = sigma.shape[2]
    sigma_blocks = sigma.reshape(2, energies, atom_count, NO, NO)
    green_blocks = green.reshape(2, energies, atom_count, NO, NO)
    gain = jnp.einsum(
        "eaij,eajk->eik", sigma_blocks[1], green_blocks[0], preferred_element_type=jnp.float32
    )
    loss = jnp.einsum(
        "eaij,eajk->eik", sigma_blocks[0], green_blocks[1], preferred_element_type=jnp.float32
    )
    return (gain - loss).reshape(energies, NO * NO)


def shards(greens, coupling, neighbours, counts, phonon_weights, offsets):
    energy_tile = lax.all_to_all(greens, "atom", split_axis=2, concat_axis=1, tiled=True)
    energies = energy_tile.shape[1]
    atom_count = energy_tile.shape[2]
    block_cells = energy_tile.shape[3]
    framed = with_halo(energy_tile, (("energy", 1), ("atom", 2)), REACH)
    framed_rows = energies + 2 * REACH
    table_less, table_greater, upward = shift_tables(phonon_weights, offsets, energies, framed_rows)
    mixed_less = jnp.einsum(
        "xy,ybc->xbc", table_less, framed[0], preferred_element_type=jnp.float32
    ).astype(jnp.bfloat16)
    mixed_greater = jnp.einsum(
        "xy,ybc->xbc", table_greater, framed[1], preferred_element_type=jnp.float32
    ).astype(jnp.bfloat16)
    sources = jnp.stack([mixed_less, mixed_greater, framed[1, REACH : REACH + energies]])
    own_less = framed[0, :, REACH : REACH + atom_count]
    atom_start = lax.axis_index("atom") * atom_count
    local_index = neighbours - atom_start + REACH
    total_energies = energies * lax.axis_size("energy")
    total_atoms = atom_count * lax.axis_size("atom")
    scale_phonon = 1.0 / math.sqrt(NO * NO * total_energies)
    scale_current = 1.0 / math.sqrt(NO * total_atoms)

    def slot_step(collected, slot_number):
        slot_index = lax.dynamic_index_in_dim(local_index, slot_number, 1, keepdims=False)
        active = (slot_number < counts).astype(jnp.float32)
        matrix = lax.dynamic_index_in_dim(coupling, slot_number, 1, keepdims=False).reshape(
            atom_count, NO, NO
        )
        gathered = jnp.take(sources, slot_index, axis=2).reshape(3, energies, atom_count, NO, NO)
        left_half = jnp.einsum(
            "aij,seajk->seaik", matrix, gathered, preferred_element_type=jnp.float32
        ).astype(jnp.bfloat16)
        sandwich = jnp.einsum(
            "seaik,alk->seail", left_half, matrix, preferred_element_type=jnp.float32
        )
        sandwich = sandwich.reshape(3, energies, atom_count, block_cells)
        collected = collected + sandwich[:2] * active[None, None, :, None]
        bubble = sandwich[2].astype(jnp.bfloat16)
        intersections = jnp.einsum(
            "xac,yac->axy", bubble, own_less, preferred_element_type=jnp.float32
        )
        phonon_term = jnp.sum(intersections[None] * upward[:, None], axis=(2, 3))
        return (collected, phonon_term * (active * scale_phonon)[None, :])

    initial = jnp.zeros((2, energies, atom_count, block_cells), jnp.float32)
    collected, terms = lax.scan(slot_step, initial, jnp.arange(NB, dtype=jnp.int32))
    self_energy = collected.astype(jnp.bfloat16)
    phonon_part = jnp.transpose(terms, (2, 0, 1)).reshape(atom_count, NB * NW)
    phonon_self = lax.psum(phonon_part, "energy")
    returned = lax.all_to_all(self_energy, "atom", split_axis=1, concat_axis=2, tiled=True)
    current = collision(returned, greens) * scale_current
    return (self_energy, phonon_self, current)


def solution(mesh):
    placed = (
        P(None, ("energy", "atom"), None, None),
        P("atom", None, None),
        P("atom", None),
        P("atom"),
        P(),
        P(),
    )
    return jax.shard_map(
        shards,
        mesh=mesh,
        in_specs=placed,
        out_specs=(P(None, "energy", "atom", None), P("atom", None), P(("energy", "atom"), None)),
        check_vma=False,
    )
```

profile of v0, /device:TPU:16, one launch (start us, length us, event | category | flops | bytes accessed | tf_op | source)
XLA Modules:
  0.0 570.3 jit_solution(5150597578065285597)
XLA Ops:
  2.3 12.6 %all-to-all-start = ((bf16[2,1,128,256]{3,0,1,2:T(2,128)(2,1)}), bf16[2,1,128,256]{3,0,1,2:T(2,128)(2,1)S(1)}, u32[]{:S(2)}, u32[]{:S(2)}) async-start(bf16[2,1,128,256]{3,0,1,2:T(2,128)(2,1)} %copy.50), calls=%async_computation | async-start | bytes 262144 | tf_op jit(solution)/shard_map/all_to_all | solution.py:56
  17.0 2.2 all-to-all-done
  26.0 15.7 %collective-permute-done.1 = bf16[2,8,16,256]{3,1,2,0:T(8,128)(2,1)S(1)} collective-permute-done((bf16[2,8,16,256]{3,1,2,0:T(8,128)(2,1)S(1)}, bf16[2,8,16,256]{3,1,2,0:T(8,128)(2,1)S(1)}, u32[]{:S(2)}, u32[]{:S(2)}) %collective-permute-start.1) | collective-permute-done | bytes 131104 | tf_op jit(solution)/shard_map/ppermute | solution.py:22
  41.8 1.9 collective-permute-start.2
  43.8 3.6 collective-permute-start.3
  52.4 173.6 %while.13 = (s32[]{:T(128)}, f32[2,8,16,256]{3,2,1,0:T(8,128)S(1)}, f32[8,16,16]{2,1,0:T(8,128)}, s32[8]{0:T(128)}, bf16[16,8,256]{2,0,1:T(8,128)(2,1)}, /*index...) while((s32[]{:T(128)}, f32[2,8,16,256]{3,2,1,0:T(8,128)S(1)}, ...), condition=%wide.region_4.5_spmd.clone, body=%wide.region_2.4_spmd.clone.sunk | while | flops 8363174 | bytes 5939213 | solution.py:101
  55.2 1.8 compare_select_fusion.8
  64.1 2.4 convolution_bitcast_fusion.4
  69.0 1.9 copy.75
  76.9 1.8 compare_select_fusion.8
  85.8 2.4 convolution_bitcast_fusion.4
  90.7 1.9 copy.75
  98.6 1.8 compare_select_fusion.8
  107.5 2.4 convolution_bitcast_fusion.4
  112.4 1.9 copy.75
  120.3 1.8 compare_select_fusion.8
  129.2 2.4 convolution_bitcast_fusion.4
  134.1 1.9 copy.75
  142.0 1.8 compare_select_fusion.8
  150.9 2.4 convolution_bitcast_fusion.4
  155.8 1.9 copy.75
  163.8 1.8 compare_select_fusion.8
  172.6 2.4 convolution_bitcast_fusion.4
  177.5 1.9 copy.75
  185.5 1.8 compare_select_fusion.8
  194.3 2.4 convolution_bitcast_fusion.4
  199.2 1.9 copy.75
  207.2 1.8 compare_select_fusion.8
  216.0 2.4 convolution_bitcast_fusion.4
  220.9 1.9 copy.75
  226.7 5.1 all-to-all-start.1
  235.3 332.3 %psum.7 = f32[16,128]{1,0:T(8,128)} all-reduce(f32[16,128]{1,0:T(8,128)S(1)} %copy.65), channel_id=1, replica_groups=mesh['energy'=96,'atom'=8] {'energy'}, use_global_device_ids=true, to_apply=%region_5.6 | all-reduce | flops 2048 | bytes 16384 | tf_op jit(solution)/shard_map/psum | solution.py:104
  (243 shorter events, 132.4 us)
Async XLA Ops:
  2.3 16.8 %all-to-all-start = ((bf16[2,1,128,256]{3,0,1,2:T(2,128)(2,1)}), bf16[2,1,128,256]{3,0,1,2:T(2,128)(2,1)S(1)}, u32[]{:S(2)}, u32[]{:S(2)}) async-start(bf16[2,1,128,256]{3,0,1,2:T(2,128)(2,1)} %copy.50), calls=%async_computation | async-start | bytes 262144 | tf_op jit(solution)/shard_map/all_to_all | solution.py:56
  19.2 6.7 %collective-permute-start = (bf16[2,8,16,256]{3,1,2,0:T(8,128)(2,1)S(1)}, bf16[2,8,16,256]{3,1,2,0:T(8,128)(2,1)S(1)}, u32[]{:S(2)}, u32[]{:S(2)}) collective-permute-start(bf16[2,8,16,256]{3,1,2,0:T(8,128)(2,1)S(1)} %copy.52), channel_id=1, source_target_pairs={{0,8},{8,16},{16,24},{24,32},{32,40},{40,48},{48,56},{56,64},{64,7... | collective-permute-start | bytes 393224 | tf_op jit(solution)/shard_map/ppermute | solution.py:21
  23.5 18.3 %collective-permute-start.1 = (bf16[2,8,16,256]{3,1,2,0:T(8,128)(2,1)S(1)}, bf16[2,8,16,256]{3,1,2,0:T(8,128)(2,1)S(1)}, u32[]{:S(2)}, u32[]{:S(2)}) collective-permute-start(bf16[2,8,16,256]{3,1,2,0:T(8,128)(2,1)S(1)} %copy.52), channel_id=1, source_target_pairs={{8,0},{16,8},{24,16},{32,24},{40,32},{48,40},{56,48},{64,56},{72,6... | collective-permute-start | bytes 393224 | tf_op jit(solution)/shard_map/ppermute | solution.py:22
  41.8 7.0 %collective-permute-start.2 = (bf16[2,24,8,256]{3,1,2,0:T(8,128)(2,1)S(1)}, bf16[2,24,8,256]{3,1,2,0:T(8,128)(2,1)S(1)}, u32[]{:S(2)}, u32[]{:S(2)}) collective-permute-start(bf16[2,24,8,256]{3,1,2,0:T(8,128)(2,1)S(1)} %get-tuple-element.174), channel_id=1, source_target_pairs={{0,1},{1,2},{2,3},{3,4},{4,5},{5,6},{6,7},{8,9},{9,10},{10,11},{11... | collective-permute-start | bytes 589832 | tf_op jit(solution)/shard_map/ppermute | solution.py:21
  43.8 6.8 %collective-permute-start.3 = (bf16[2,24,8,256]{3,1,2,0:T(8,128)(2,1)S(1)}, bf16[2,24,8,256]{3,1,2,0:T(8,128)(2,1)S(1)}, u32[]{:S(2)}, u32[]{:S(2)}) collective-permute-start(bf16[2,24,8,256]{3,1,2,0:T(8,128)(2,1)S(1)} %get-tuple-element.175), channel_id=1, source_target_pairs={{1,0},{2,1},{3,2},{4,3},{5,4},{6,5},{7,6},{9,8},{10,9},{11,10},{12... | collective-permute-start | bytes 589832 | tf_op jit(solution)/shard_map/ppermute | solution.py:22
  50.7 1.7 copy-start.2
  70.9 1.1 copy-start
  71.8 1.0 copy-start.1
  71.8 1.6 copy-start.3
  92.6 1.1 copy-start
  93.5 1.0 copy-start.1
  93.6 1.6 copy-start.3
  114.3 1.1 copy-start
  115.2 1.0 copy-start.1
  115.2 1.6 copy-start.3
  136.0 1.1 copy-start
  136.9 1.0 copy-start.1
  137.0 1.6 copy-start.3
  157.7 1.1 copy-start
  158.7 1.0 copy-start.1
  158.7 1.6 copy-start.3
  179.4 1.1 copy-start
  180.4 1.0 copy-start.1
  180.4 1.6 copy-start.3
  201.1 1.1 copy-start
  202.1 1.0 copy-start.1
  202.1 1.6 copy-start.3
  222.8 1.1 copy-start
  223.8 1.0 copy-start.1
  223.8 1.6 copy-start.3
  226.7 341.0 %all-to-all-start.1 = ((bf16[2,8,16,256]{3,2,0,1:T(8,128)(2,1)}), bf16[2,8,16,256]{3,2,0,1:T(8,128)(2,1)S(1)}, u32[]{:S(2)}, u32[]{:S(2)}) async-start(bf16[2,8,16,256]{3,2,0,1:T(8,128)(2,1)} %copy.70), calls=%async_computation.1 | async-start | bytes 262144 | tf_op jit(solution)/shard_map/all_to_all | solution.py:105
where the time goes:
time: 573 us; the launch traced here: 570 us
  blocking collectives  332 us (58%)
  local copies, waits for them, and re-layouts  110 us (19%)
  other arithmetic  43.7 us (8%)
  starting transfers between devices  25.8 us (5%)
  waiting for transfers between devices  21.6 us (4%)
  matrix products  21.4 us (4%)
  loops' own time  14.3 us (2%)
    psum x1, blocking collectives, shards(): phonon_self = lax.psum(phonon_part, 'energy')  332 us
    slice x24, local copies, waits for them, and re-layouts, slot_step(): collected = collected + sandwich[:2] * active[None, None, :, None]  35.1 us
    gather x24, local copies, waits for them, and re-layouts, slot_step(): jnp.take(sources, slot_index, axis=2)  33.7 us
    dot_general x8, matrix products, slot_step(): jnp.einsum('seaik,alk->seail', left_half, matrix, preferred_element_type=...  19.5 us
    ppermute x2, waiting for transfers between devices, with_halo(): after = lax.ppermute(leading, axis, down)  17.5 us
    mul x8, other arithmetic, slot_step(): return (collected, phonon_term * (active * scale_phonon)[None, :])  14.4 us
    another operation x1, loops' own time, shards(): lax.scan(slot_step, initial, jnp.arange(NB, dtype=jnp.int32))  14.3 us
    all_to_all x1, starting transfers between devices, shards(): lax.all_to_all(greens, 'atom', split_axis=2, concat_axis=1, tiled=True)  12.6 us
  transfers between devices with their start and end apart: 6, of which 5 were waited for; matrix products, arithmetic and copies ran while one was open for 2% of the time, Pallas kernels for 0%

commit v1 on v0

v1 whole, which is shorter than its diff:
```python
import math

import jax
import jax.numpy as jnp
from jax import lax
from jax.experimental import pallas as pl
from jax.experimental.pallas import tpu as pltpu
from jax.sharding import Mesh
from jax.sharding import PartitionSpec as P

NO = 16
NB = 8
NW = 16
REACH = 8
CELLS = NO * NO
BF16 = jnp.bfloat16
F32 = jnp.float32
GRID = ("x", "z", "h", "atom")

VMEM = pl.BlockSpec(memory_space=pltpu.VMEM)
SMEM = pl.BlockSpec(memory_space=pltpu.SMEM)
PARAMS = pltpu.CompilerParams(vmem_limit_bytes=12 * 1024 * 1024)


def iota(shape, axis):
    return lax.broadcasted_iota(jnp.int32, shape, axis)


def window_kernel(greens, out):
    windows = out.shape[0] // 2
    blank = jnp.zeros((8, CELLS), BF16)
    for h in range(2):
        for w in range(windows):
            for field in range(2):
                begin, end = w * 16 - 8, w * 16 + 24
                d = h * windows + w
                if w == 0:
                    out[d, field, 0:8] = blank
                    out[d, field, 8:32] = greens[field, 0, 0:end]
                elif w == windows - 1:
                    out[d, field, 0:24] = greens[field, 0, begin : end - 8]
                    out[d, field, 24:32] = blank
                else:
                    out[d, field] = greens[field, 0, begin:end]


def spread_kernel(neighbours, coupling, spread, tiled, index):
    row, col = iota((CELLS, CELLS), 0), iota((CELLS, CELLS), 1)
    pick_spread = (row // NO == col // NO).astype(F32).astype(BF16)
    pick_tiled = (row // NO == col % NO).astype(F32).astype(BF16)
    keep = iota((NO, CELLS), 0) == iota((NO, CELLS), 1) % NO
    shift = 8 - lax.axis_index("atom") * 16
    for a in range(coupling.shape[0]):
        for n in range(NB):
            index[a * NB + n] = neighbours[a, n] + shift

    def atom(a, carry):
        block = coupling[a].astype(F32)
        lines = [jnp.where(keep, block[n : n + 1], 0.0) for n in range(NB)]
        lines = jnp.concatenate(lines, axis=0).astype(BF16)
        first = jnp.dot(lines, pick_spread, preferred_element_type=F32)
        second = jnp.dot(lines, pick_tiled, preferred_element_type=F32)
        spread[a] = first.astype(BF16).reshape(NB, NO, CELLS)
        tiled[a] = second.astype(BF16).reshape(NB, NO, CELLS)
        return carry

    lax.fori_loop(0, coupling.shape[0], atom, 0)


def kron_rows(spread, tiled):
    product = spread.astype(F32)[:, None, :] * tiled.astype(F32)[None, :, :]
    return product.reshape(CELLS, CELLS).astype(BF16)


def bubble_kernel(index, spread, tiled, tile, out):
    first = lax.axis_index("h") * 8

    def atom(a, carry):
        for n in range(NB):
            matrix = kron_rows(spread[first + a, n], tiled[first + a, n])
            block = tile[1, index[(first + a) * NB + n]]
            product = jnp.dot(block, matrix, preferred_element_type=F32)
            out[a, n * 16 : n * 16 + 16] = product.astype(BF16)
        return carry

    lax.fori_loop(0, 8, atom, 0)


def overlap_kernel(bubble, tile, upper, out, frame, terms):
    first = lax.axis_index("h") * 8 + 8
    frame[...] = jnp.zeros_like(frame)
    distance = iota((32, NB * 16), 0) - iota((32, NB * 16), 1) % 16
    for a in range(8):
        frame[a, 0:16] = tile[0, first + a]
        frame[a, 16:24] = upper[a]
        overlap = lax.dot_general(
            frame[a], bubble[a], (((1,), (1,)), ((), ())), preferred_element_type=F32
        )
        parts = []
        for d in range(1, REACH + 1):
            parts.append(jnp.sum(jnp.where(distance == d, overlap, 0.0), axis=0, keepdims=True))
        terms[a] = jnp.concatenate(parts, axis=0)
    column = iota((NB * 16, NB * REACH), 1)
    gather = (iota((NB * 16, NB * REACH), 0) // 16 == column // REACH).astype(F32)
    sums = jnp.dot(
        terms[...].reshape(8 * REACH, NB * 16),
        gather,
        preferred_element_type=F32,
        precision=lax.Precision.HIGHEST,
    ).reshape(8, REACH, NB * REACH)
    same = iota((REACH, NB * REACH), 0) == iota((REACH, NB * REACH), 1) % REACH
    total = jnp.sum(jnp.where(same[None], sums, 0.0), axis=1)
    total = jnp.concatenate([total[0:4], total[4:8]], axis=1)
    for copy in range(out.shape[0]):
        out[copy] = total


def combine_kernel(parts, current, out):
    half = lax.axis_index("h")
    total = parts[0]
    for column in range(1, parts.shape[0]):
        total = total + parts[column]
    owners = current.shape[0]
    for h in range(2):
        mine = (half == h).astype(F32)
        for a in range(owners):
            d = h * owners + a
            out[d, 0:1] = current[a : a + 1, 0:128] * mine
            out[d, 1:2] = current[a : a + 1, 128:256] * mine
            out[d, 2:6] = total
            out[d, 6:8] = jnp.zeros((2, 128), F32)


def final_kernel(scale_phonon, scale_current, counts, offsets, received, phonon, current):
    atom = lax.axis_index("atom")
    owners = received.shape[0] // 2
    total = received[0]
    for source in range(1, received.shape[0]):
        total = total + received[source]
    current[0:1, 0:128] = total[0:1] * scale_current
    current[0:1, 128:256] = total[1:2] * scale_current
    sums = jnp.concatenate([received[atom, 2:6], received[owners + atom, 2:6]], axis=0)
    row, col = iota((128, 128), 0), iota((128, 128), 1)
    wanted = jnp.zeros((128, 128), jnp.int32)
    for w in range(NW):
        wanted = jnp.where(col % NW == w, offsets[w], wanted)
    slot = (row % 64) // REACH == col // NW
    match = slot & (row % REACH + 1 == wanted)
    pieces = []
    for side in range(2):
        expand = (match & (row // 64 == side)).astype(F32)
        pieces.append(
            jnp.dot(sums, expand, preferred_element_type=F32, precision=lax.Precision.HIGHEST)
        )
    values = jnp.concatenate([pieces[0][0:4], pieces[1][0:4], pieces[0][4:8], pieces[1][4:8]], axis=0)
    live = jnp.zeros((16, NB * NW), jnp.int32)
    line = iota((16, NB * NW), 0)
    for a in range(16):
        live = jnp.where(line == a, counts[a], live)
    phonon[...] = jnp.where(iota((16, NB * NW), 1) // NW < live, values * scale_phonon, 0.0)


def mix_table(phonon_weights, offsets, half):
    row, col = iota((16, 48), 0), iota((16, 48), 1)
    row_field, row_energy = row // 8, row % 8 + 8 * half
    inside = col < 32
    col_field = jnp.where(inside, col // 16, (col - 32) // 8)
    outer = jnp.where(half == 0, -8, 16)
    col_energy = jnp.where(inside, col % 16, col % 8 + outer)
    step = col_energy - row_energy
    step = jnp.where(row_field == 0, step, -step)
    table = jnp.zeros((16, 48), F32)
    for w in range(NW):
        table = table + jnp.where(step == offsets[w], phonon_weights[0, w], 0.0)
        table = table + jnp.where(step == -offsets[w], phonon_weights[1, w], 0.0)
    return jnp.where(row_field == col_field, table, 0.0).astype(BF16)


def energy_kernel(index, counts, offsets, weights, spread, tiled, tile, ring, out, mixed):
    table = mix_table(weights, offsets, lax.axis_index("h"))
    for a in range(mixed.shape[0]):
        frame = jnp.concatenate([tile[0, a], tile[1, a], ring[a]], axis=0)
        mixed[a] = jnp.dot(table, frame, preferred_element_type=F32).astype(BF16)

    def atom(a, carry):
        total = jnp.zeros((NO, CELLS), F32)
        for n in range(NB):
            matrix = kron_rows(spread[a, n], tiled[a, n])
            block = mixed[index[a * NB + n]]
            live = (n < counts[a]).astype(F32)
            total = total + live * jnp.dot(block, matrix, preferred_element_type=F32)
        out[a] = total.astype(BF16)
        return carry

    lax.fori_loop(0, out.shape[0], atom, 0)


def links(nx, nz, na, target):
    pairs = []
    for column in range(nx * nz):
        for h in range(2):
            for a in range(na):
                to, h_to, a_to = target(column, h, a)
                if 0 <= to < nx * nz and 0 <= a_to < na:
                    pairs.append(((column * 2 + h) * na + a, (to * 2 + h_to) * na + a_to))
    return pairs


def collision(sigma, green):
    sigma_blocks = sigma.reshape(2, 8, 16, NO, NO)
    green_blocks = green.reshape(2, 8, 16, NO, NO)
    gain = jnp.einsum(
        "eaij,eajk->eik", sigma_blocks[1], green_blocks[0], preferred_element_type=F32
    )
    loss = jnp.einsum(
        "eaij,eajk->eik", sigma_blocks[0], green_blocks[1], preferred_element_type=F32
    )
    return (gain - loss).reshape(8, CELLS)


def cost(flops, size):
    return pl.CostEstimate(flops=flops, bytes_accessed=size, transcendentals=0)


def shards(nx, nz, na, greens, coupling, neighbours, counts, phonon_weights, offsets):
    half = lax.axis_index("h")
    scale_phonon = 1.0 / math.sqrt(CELLS * nx * nz * 16)
    scale_current = 1.0 / math.sqrt(NO * na * 16)

    windows = pl.pallas_call(
        window_kernel,
        out_shape=jax.ShapeDtypeStruct((2 * na, 2, 32, CELLS), BF16),
        in_specs=[VMEM],
        out_specs=VMEM,
        compiler_params=PARAMS,
        cost_estimate=cost(1000, 700_000),
    )(greens)
    received = lax.all_to_all(windows, ("h", "atom"), split_axis=0, concat_axis=0, tiled=True)
    table_shape = jax.ShapeDtypeStruct((16, NB, NO, CELLS), BF16)
    spread, tiled, index = pl.pallas_call(
        spread_kernel,
        out_shape=(table_shape, table_shape, jax.ShapeDtypeStruct((16 * NB,), jnp.int32)),
        in_specs=[SMEM, VMEM],
        out_specs=(VMEM, VMEM, SMEM),
        compiler_params=PARAMS,
        cost_estimate=cost(500_000_000, 3_000_000),
    )(neighbours, coupling)

    tile = jnp.transpose(received, (1, 2, 0, 3))
    tile, spread, tiled, index = lax.optimization_barrier((tile, spread, tiled, index))
    above = lax.dynamic_slice_in_dim(tile[0, :, 0:8], 8 * half + 8, 8, 0)
    upper = lax.ppermute(above, GRID, links(nx, nz, na, lambda c, h, a: (c - 1, h, a)))
    edge = lax.dynamic_slice_in_dim(tile, 8 * (1 - half), 8, 2)
    edge = jnp.swapaxes(edge, 0, 1).reshape(32, 16, CELLS)
    ring = lax.ppermute(edge, GRID, links(nx, nz, na, lambda c, h, a: (c + 1 - 2 * h, h, a)))

    bubble = pl.pallas_call(
        bubble_kernel,
        out_shape=jax.ShapeDtypeStruct((8, NB * 16, CELLS), BF16),
        in_specs=[SMEM] + [VMEM] * 3,
        out_specs=VMEM,
        compiler_params=PARAMS,
        cost_estimate=cost(400_000_000, 4_000_000),
        name="bubble",
    )(index, spread, tiled, tile)
    phonon_part = pl.pallas_call(
        overlap_kernel,
        out_shape=jax.ShapeDtypeStruct((nx * nz, 4, 128), F32),
        in_specs=[VMEM] * 3,
        out_specs=VMEM,
        scratch_shapes=[pltpu.VMEM((8, 32, CELLS), BF16), pltpu.VMEM((8, REACH, NB * 16), F32)],
        compiler_params=PARAMS,
        cost_estimate=cost(40_000_000, 1_000_000),
        name="overlap",
    )(bubble, tile, upper)
    parts = lax.all_to_all(phonon_part, ("x", "z"), split_axis=0, concat_axis=0, tiled=True)

    ring_later, tile_later, _ = lax.optimization_barrier((ring, tile, phonon_part))
    own = jnp.swapaxes(lax.dynamic_slice_in_dim(tile_later[:, 8:24], 8 * half, 8, 2), 1, 2)
    sigma = pl.pallas_call(
        energy_kernel,
        out_shape=jax.ShapeDtypeStruct((16, 16, CELLS), BF16),
        in_specs=[SMEM] * 4 + [VMEM] * 4,
        out_specs=VMEM,
        scratch_shapes=[pltpu.VMEM((32, 16, CELLS), BF16)],
        cost_estimate=cost(800_000_000, 4_000_000),
        compiler_params=PARAMS,
        name="energy",
    )(index, counts, offsets, phonon_weights, spread, tiled, tile_later, ring_later)
    self_energy = jnp.transpose(sigma, (1, 0, 2)).reshape(2, 8, 16, CELLS)
    current_part = collision(self_energy, own)
    message = pl.pallas_call(
        combine_kernel,
        out_shape=jax.ShapeDtypeStruct((2 * na, 8, 128), F32),
        in_specs=[VMEM, VMEM],
        out_specs=VMEM,
        compiler_params=PARAMS,
        name="combine",
    )(parts, current_part)
    received_sums = lax.all_to_all(message, ("h", "atom"), split_axis=0, concat_axis=0, tiled=True)
    phonon_self, current = pl.pallas_call(
        lambda *refs: final_kernel(scale_phonon, scale_current, *refs),
        out_shape=(
            jax.ShapeDtypeStruct((16, NB * NW), F32),
            jax.ShapeDtypeStruct((1, CELLS), F32),
        ),
        in_specs=[SMEM, SMEM, VMEM],
        out_specs=(VMEM, VMEM),
        compiler_params=PARAMS,
        name="final",
    )(counts, offsets, received_sums)
    return (self_energy, phonon_self, current)


def solution(mesh):
    na = mesh.shape["atom"]
    nz = 12
    nx = mesh.shape["energy"] // (2 * nz)
    grid = Mesh(mesh.devices.reshape(nx, nz, 2, na), GRID)
    placed = (
        P(None, GRID, None, None),
        P("atom", None, None),
        P("atom", None),
        P("atom"),
        P(),
        P(),
    )

    def body(*args):
        return shards(nx, nz, na, *args)

    return jax.shard_map(
        body,
        mesh=grid,
        in_specs=placed,
        out_specs=(P(None, ("x", "z", "h"), "atom", None), P("atom", None), P(GRID, None)),
        check_vma=False,
    )
```

time: 573 us -> 88 us (0.15)
  the two profiles are of different devices: /device:TPU:16 before, /device:TPU:1 now
where the time goes in v1:
time: 88 us; the launch traced here: 87.5 us
  starting transfers between devices  39.9 us (45%)
  waiting for transfers between devices  22.9 us (26%)
  Pallas kernels  16.9 us (19%)
  local copies, waits for them, and re-layouts  6.03 us (7%)
    all_to_all x1, starting transfers between devices, shards(): lax.all_to_all(phonon_part, ('x', 'z'), split_axis=0, concat_axis=0, tile...  15.1 us
    all_to_all x1, starting transfers between devices, shards(): lax.all_to_all(windows, ('h', 'atom'), split_axis=0, concat_axis=0, tiled...  14.6 us
    all_to_all x1, waiting for transfers between devices, shards(): lax.all_to_all(windows, ('h', 'atom'), split_axis=0, concat_axis=0, tiled...  12.4 us
    all_to_all x1, starting transfers between devices, shards(): lax.all_to_all(message, ('h', 'atom'), split_axis=0, concat_axis=0, tiled...  7.66 us
    all_to_all x1, waiting for transfers between devices, shards(): lax.all_to_all(message, ('h', 'atom'), split_axis=0, concat_axis=0, tiled...  7.08 us
    pallas_call x1, Pallas kernels, shards(): pl.pallas_call(energy_kernel, out_shape=jax.ShapeDtypeStruct((16, 16, CEL...  5.62 us
    pallas_call x1, Pallas kernels, shards(): pl.pallas_call(spread_kernel, out_shape=(table_shape, table_shape, jax.Sh...  4.26 us
    all_to_all x1, waiting for transfers between devices, shards(): lax.all_to_all(phonon_part, ('x', 'z'), split_axis=0, concat_axis=0, tile...  3.02 us
  transfers between devices with their start and end apart: 5, of which 4 were waited for; matrix products, arithmetic and copies ran while one was open for 4% of the time, Pallas kernels for 16%

profile of v1, /device:TPU:1, one launch (start us, length us, event | category | flops | bytes accessed | tf_op | source)
XLA Modules:
  0.0 87.5 jit_solution(17914993674865406847)
XLA Ops:
  0.6 0.9 %copy-done = bf16[2,1,128,256]{3,2,1,0:T(8,128)(2,1)S(1)} copy-done((bf16[2,1,128,256]{3,2,1,0:T(8,128)(2,1)S(1)}, bf16[2,1,128,256]{3,2,1,0:T(8,128)(2,1)}, u32[]{:S(2)}) %copy-start) | copy-done | bytes 131096
  1.5 0.8 shard_map.85
  2.4 14.6 %all-to-all-start = ((bf16[16,2,32,256]{3,2,1,0:T(8,128)(2,1)}), bf16[16,2,32,256]{3,2,1,0:T(8,128)(2,1)}, u32[]{:S(2)}, u32[]{:S(2)}) async-start(bf16[16,2,32,256]{3,2,1,0:T(8,128)(2,1)} %shard_map.85), calls=%async_computation | async-start | bytes 1048576 | tf_op jit(solution)/shard_map/all_to_all | solution.py:238
  17.0 0.7 copy-done.5
  17.6 0.1 copy.18.neighbours
  17.7 4.3 %shard_map.86 = (bf16[16,8,16,256]{3,2,1,0:T(8,128)(2,1)S(1)}, bf16[16,8,16,256]{3,2,1,0:T(8,128)(2,1)S(1)}, s32[128]{0:T(128)S(1)}) custom-call(s32[16,8]{1,0:T(8,128)S(1)} %copy.18.neighbours, bf16[16,8,256]{2,1,0:T(8,128)(2,1)S(1)} %copy-done.4), custom_call_target="tpu_custom_call" | custom-call | flops 500000000 | bytes 3000000 | tf_op jit(solution)/shard_map/pallas_call | solution.py:240
  22.0 12.4 %all-to-all-done = bf16[16,2,32,256]{3,2,1,0:T(8,128)(2,1)} async-done(((bf16[16,2,32,256]{3,2,1,0:T(8,128)(2,1)}), bf16[16,2,32,256]{3,2,1,0:T(8,128)(2,1)}, u32[]{:S(2)}, u32[]{:S(2)}) %all-to-all-start) | async-done | bytes 524320 | tf_op jit(solution)/shard_map/all_to_all | solution.py:238
  34.4 1.3 %copy.31 = bf16[16,2,32,256]{3,0,2,1:T(8,128)(2,1)S(1)} copy(bf16[16,2,32,256]{3,2,1,0:T(8,128)(2,1)} %all-to-all-done) | data formatting | bytes 1048576 | tf_op jit(solution)/shard_map/all_to_all | solution.py:238
  35.7 1.3 %collective-permute-start = (bf16[32,16,256]{2,1,0:T(8,128)(2,1)S(1)}, bf16[32,16,256]{2,1,0:T(8,128)(2,1)S(1)}, u32[]{:S(2)}, u32[]{:S(2)}) collective-permute-start(bf16[32,16,256]{2,1,0:T(8,128)(2,1)S(1)} %copy_bitcast_fusion.1), channel_id=1, source_target_pairs={{0,16},{1,17},{2,18},{3,19},{4,20},{5,21},{6,22},{7,23},{16,32},{1... | collective-permute-start | bytes 786440 | tf_op jit(solution)/shard_map/ppermute | solution.py:255
  37.1 1.3 %collective-permute-start.1 = (bf16[8,8,256]{2,1,0:T(8,128)(2,1)S(1)}, bf16[8,8,256]{2,1,0:T(8,128)(2,1)S(1)}, u32[]{:S(2)}, u32[]{:S(2)}) collective-permute-start(bf16[8,8,256]{2,1,0:T(8,128)(2,1)S(1)} %dynamic-slice_bitcast_fusion.2), channel_id=1, source_target_pairs={{16,0},{17,1},{18,2},{19,3},{20,4},{21,5},{22,6},{23,7},{24,8},{25... | collective-permute-start | bytes 98312 | tf_op jit(solution)/shard_map/ppermute | solution.py:252
  38.4 2.9 %bubble.1 = bf16[8,128,256]{2,1,0:T(8,128)(2,1)S(1)} custom-call(s32[128]{0:T(128)S(1)} %get-tuple-element.17.index, bf16[16,8,16,256]{3,2,1,0:T(8,128)(2,1)S(1)} %get-tuple-element.18.spread, bf16[16,8,16,256]{3,2,1,0:T(8,128)(2,1)S(1)} %get-tuple-element.19.tiled, bf16[2,32,16,256]{3,2,1,0:T(8,128)(2,1)S(1)} %bitcast.39), custom_call_target="tpu_custom_call" | custom-call | flops 400000000 | bytes 4000000 | tf_op jit(solution)/shard_map/bubble/pallas_call | solution.py:257
  41.3 0.4 collective-permute-done.1.upper
  41.8 1.2 %overlap.1 = f32[48,4,128]{2,1,0:T(4,128)} custom-call(bf16[8,128,256]{2,1,0:T(8,128)(2,1)S(1)} %bubble.1, bf16[2,32,16,256]{3,2,1,0:T(8,128)(2,1)S(1)} %bitcast.40, bf16[8,8,256]{2,1,0:T(8,128)(2,1)S(1)} %collective-permute-done.1.upper), custom_call_target="tpu_custom_call" | custom-call | flops 40000000 | bytes 1000000 | tf_op jit(solution)/shard_map/overlap/pallas_call | solution.py:266
  43.0 15.1 %all-to-all-start.1 = ((f32[48,4,128]{2,1,0:T(4,128)}), f32[48,4,128]{2,1,0:T(4,128)S(1)}, u32[]{:S(2)}, u32[]{:S(2)}) async-start(f32[48,4,128]{2,1,0:T(4,128)} %overlap.1), calls=%async_computation.1 | async-start | bytes 196608 | tf_op jit(solution)/shard_map/all_to_all | solution.py:276
  58.1 0.0 copy-start.1
  58.2 0.6 copy-done.1
  58.8 0.0 copy-done.2
  58.8 0.0 copy-done.3
  58.8 5.6 %energy.1 = bf16[16,16,256]{2,1,0:T(8,128)(2,1)S(1)} custom-call(s32[128]{0:T(128)S(1)} %get-tuple-element.17.index, s32[16]{0:T(128)S(1)} %copy-done.1, s32[16]{0:T(128)S(1)} %copy-done.2, f32[2,16]{1,0:T(2,128)S(1)} %copy-done.3, bf16[16,8,16,256]{3,2,1,0:T(8,128)(2,1)S(1)} %get-tuple-element.18.spread, ...), custom_call_target="tpu_custom_call" | custom-call | flops 800000000 | bytes 4000000 | tf_op jit(solution)/shard_map/energy/pallas_call | solution.py:280
  64.5 0.4 squeeze.15
  64.9 0.4 squeeze.16
  65.2 0.4 convolution_bitcast_fusion
  65.6 0.4 squeeze.13
  66.0 0.4 squeeze.14
  66.4 0.4 fusion
  66.8 0.1 reshape.27.current
  66.9 3.0 %all-to-all-done.1.parts = f32[48,4,128]{2,1,0:T(4,128)S(1)} async-done(((f32[48,4,128]{2,1,0:T(4,128)}), f32[48,4,128]{2,1,0:T(4,128)S(1)}, u32[]{:S(2)}, u32[]{:S(2)}) %all-to-all-start.1) | async-done | bytes 98336 | tf_op jit(solution)/shard_map/all_to_all | solution.py:276
  70.0 0.7 combine.1
  70.6 7.7 %all-to-all-start.2 = ((f32[16,8,128]{2,1,0:T(8,128)}), f32[16,8,128]{2,1,0:T(8,128)S(1)}, u32[]{:S(2)}, u32[]{:S(2)}) async-start(f32[16,8,128]{2,1,0:T(8,128)} %combine.1), calls=%async_computation.2 | async-start | bytes 131072 | tf_op jit(solution)/shard_map/all_to_all | solution.py:300
  78.3 0.7 copy.24
  79.0 7.1 %all-to-all-done.2.refs_2_ = f32[16,8,128]{2,1,0:T(8,128)S(1)} async-done(((f32[16,8,128]{2,1,0:T(8,128)}), f32[16,8,128]{2,1,0:T(8,128)S(1)}, u32[]{:S(2)}, u32[]{:S(2)}) %all-to-all-start.2) | async-done | bytes 65568 | tf_op jit(solution)/shard_map/all_to_all | solution.py:300
  86.1 1.4 %final.1 = (f32[16,128]{1,0:T(8,128)}, f32[1,256]{1,0:T(1,128)}) custom-call(s32[16]{0:T(128)S(1)} %copy-done.1, s32[16]{0:T(128)S(1)} %copy-done.2, f32[16,8,128]{2,1,0:T(8,128)S(1)} %all-to-all-done.2.refs_2_), custom_call_target="tpu_custom_call" | custom-call | tf_op jit(solution)/shard_map/final/pallas_call | solution.py:301
  (14 shorter events, 0.1 us)
Async XLA Ops:
  0.6 0.9 %copy-start = (bf16[2,1,128,256]{3,2,1,0:T(8,128)(2,1)S(1)}, bf16[2,1,128,256]{3,2,1,0:T(8,128)(2,1)}, u32[]{:S(2)}) copy-start(bf16[2,1,128,256]{3,2,1,0:T(8,128)(2,1)} %greens.1) | copy-start | bytes 393220
  2.4 15.3 %copy-start.4 = (bf16[16,8,256]{2,1,0:T(8,128)(2,1)S(1)}, bf16[16,8,256]{2,1,0:T(8,128)(2,1)}, u32[]{:S(2)}) copy-start(bf16[16,8,256]{2,1,0:T(8,128)(2,1)} %coupling.1) | copy-start | bytes 196612
  2.4 32.0 %all-to-all-start = ((bf16[16,2,32,256]{3,2,1,0:T(8,128)(2,1)}), bf16[16,2,32,256]{3,2,1,0:T(8,128)(2,1)}, u32[]{:S(2)}, u32[]{:S(2)}) async-start(bf16[16,2,32,256]{3,2,1,0:T(8,128)(2,1)} %shard_map.85), calls=%async_computation | async-start | bytes 1048576 | tf_op jit(solution)/shard_map/all_to_all | solution.py:238
  16.9 0.7 copy-start.5
  35.7 22.3 %collective-permute-start = (bf16[32,16,256]{2,1,0:T(8,128)(2,1)S(1)}, bf16[32,16,256]{2,1,0:T(8,128)(2,1)S(1)}, u32[]{:S(2)}, u32[]{:S(2)}) collective-permute-start(bf16[32,16,256]{2,1,0:T(8,128)(2,1)S(1)} %copy_bitcast_fusion.1), channel_id=1, source_target_pairs={{0,16},{1,17},{2,18},{3,19},{4,20},{5,21},{6,22},{7,23},{16,32},{1... | collective-permute-start | bytes 786440 | tf_op jit(solution)/shard_map/ppermute | solution.py:255
  37.1 4.7 %collective-permute-start.1 = (bf16[8,8,256]{2,1,0:T(8,128)(2,1)S(1)}, bf16[8,8,256]{2,1,0:T(8,128)(2,1)S(1)}, u32[]{:S(2)}, u32[]{:S(2)}) collective-permute-start(bf16[8,8,256]{2,1,0:T(8,128)(2,1)S(1)} %dynamic-slice_bitcast_fusion.2), channel_id=1, source_target_pairs={{16,0},{17,1},{18,2},{19,3},{20,4},{21,5},{22,6},{23,7},{24,8},{25... | collective-permute-start | bytes 98312 | tf_op jit(solution)/shard_map/ppermute | solution.py:252
  43.0 27.0 %all-to-all-start.1 = ((f32[48,4,128]{2,1,0:T(4,128)}), f32[48,4,128]{2,1,0:T(4,128)S(1)}, u32[]{:S(2)}, u32[]{:S(2)}) async-start(f32[48,4,128]{2,1,0:T(4,128)} %overlap.1), calls=%async_computation.1 | async-start | bytes 196608 | tf_op jit(solution)/shard_map/all_to_all | solution.py:276
  58.1 0.7 copy-start.1
  58.1 0.7 copy-start.2
  58.1 0.7 copy-start.3
  70.6 15.4 %all-to-all-start.2 = ((f32[16,8,128]{2,1,0:T(8,128)}), f32[16,8,128]{2,1,0:T(8,128)S(1)}, u32[]{:S(2)}, u32[]{:S(2)}) async-start(f32[16,8,128]{2,1,0:T(8,128)} %combine.1), calls=%async_computation.2 | async-start | bytes 131072 | tf_op jit(solution)/shard_map/all_to_all | solution.py:300

commit v2 on v1

--- a/solution.py
+++ b/solution.py
@@ -7,6 +7,7 @@
 from jax.experimental.pallas import tpu as pltpu
 from jax.sharding import Mesh
 from jax.sharding import PartitionSpec as P
+
 
 NO = 16
 NB = 8
@@ -47,7 +48,7 @@
 def spread_kernel(neighbours, coupling, spread, tiled, index):
     row, col = iota((CELLS, CELLS), 0), iota((CELLS, CELLS), 1)
     pick_spread = (row // NO == col // NO).astype(F32).astype(BF16)
-    pick_tiled = (row // NO == col % NO).astype(F32).astype(BF16)
+    pick_tiled = (row // NO == col % NO).astype(F32).astype(BF16)[:, 0:128]
     keep = iota((NO, CELLS), 0) == iota((NO, CELLS), 1) % NO
     shift = 8 - lax.axis_index("atom") * 16
     for a in range(coupling.shape[0]):
@@ -61,19 +62,21 @@
         first = jnp.dot(lines, pick_spread, preferred_element_type=F32)
         second = jnp.dot(lines, pick_tiled, preferred_element_type=F32)
         spread[a] = first.astype(BF16).reshape(NB, NO, CELLS)
-        tiled[a] = second.astype(BF16).reshape(NB, NO, CELLS)
+        tiled[a] = second.astype(BF16).reshape(NB, NO, 128)
         return carry
 
     lax.fori_loop(0, coupling.shape[0], atom, 0)
 
 
 def kron_rows(spread, tiled):
+    tiled = jnp.concatenate([tiled, tiled], axis=1)
     product = spread.astype(F32)[:, None, :] * tiled.astype(F32)[None, :, :]
     return product.reshape(CELLS, CELLS).astype(BF16)
 
 
-def bubble_kernel(index, spread, tiled, tile, out):
-    first = lax.axis_index("h") * 8
+def bubble_kernel(index, spread, tiled, tile, out, edge):
+    half = lax.axis_index("h")
+    first = half * 8
 
     def atom(a, carry):
         for n in range(NB):
@@ -84,6 +87,10 @@
         return carry
 
     lax.fori_loop(0, 8, atom, 0)
+    for b in range(tile.shape[1]):
+        for field in range(2):
+            kept = jnp.where(half == 0, tile[field, b, 8:16], tile[field, b, 0:8])
+            edge[b, field * 8 : field * 8 + 8] = kept
 
 
 def overlap_kernel(bubble, tile, upper, out, frame, terms):
@@ -222,6 +229,21 @@
     return pl.CostEstimate(flops=flops, bytes_accessed=size, transcendentals=0)
 
 
+def sandwich(index, spread, tiled, tile):
+    return pl.pallas_call(
+        bubble_kernel,
+        out_shape=(
+            jax.ShapeDtypeStruct((8, NB * 16, CELLS), BF16),
+            jax.ShapeDtypeStruct((32, 16, CELLS), BF16),
+        ),
+        in_specs=[SMEM] + [VMEM] * 3,
+        out_specs=(VMEM, VMEM),
+        compiler_params=PARAMS,
+        cost_estimate=cost(400_000_000, 4_000_000),
+        name="bubble",
+    )(index, spread, tiled, tile)
+
+
 def shards(nx, nz, na, greens, coupling, neighbours, counts, phonon_weights, offsets):
     half = lax.axis_index("h")
     scale_phonon = 1.0 / math.sqrt(CELLS * nx * nz * 16)
@@ -236,10 +258,13 @@
         cost_estimate=cost(1000, 700_000),
     )(greens)
     received = lax.all_to_all(windows, ("h", "atom"), split_axis=0, concat_axis=0, tiled=True)
-    table_shape = jax.ShapeDtypeStruct((16, NB, NO, CELLS), BF16)
     spread, tiled, index = pl.pallas_call(
         spread_kernel,
-        out_shape=(table_shape, table_shape, jax.ShapeDtypeStruct((16 * NB,), jnp.int32)),
+        out_shape=(
+            jax.ShapeDtypeStruct((16, NB, NO, CELLS), BF16),
+            jax.ShapeDtypeStruct((16, NB, NO, 128), BF16),
+            jax.ShapeDtypeStruct((16 * NB,), jnp.int32),
+        ),
         in_specs=[SMEM, VMEM],
         out_specs=(VMEM, VMEM, SMEM),
         compiler_params=PARAMS,
@@ -250,19 +275,8 @@
     tile, spread, tiled, index = lax.optimization_barrier((tile, spread, tiled, index))
     above = lax.dynamic_slice_in_dim(tile[0, :, 0:8], 8 * half + 8, 8, 0)
     upper = lax.ppermute(above, GRID, links(nx, nz, na, lambda c, h, a: (c - 1, h, a)))
-    edge = lax.dynamic_slice_in_dim(tile, 8 * (1 - half), 8, 2)
-    edge = jnp.swapaxes(edge, 0, 1).reshape(32, 16, CELLS)
+    bubble, edge = sandwich(index, spread, tiled, tile)
     ring = lax.ppermute(edge, GRID, links(nx, nz, na, lambda c, h, a: (c + 1 - 2 * h, h, a)))
-
-    bubble = pl.pallas_call(
-        bubble_kernel,
-        out_shape=jax.ShapeDtypeStruct((8, NB * 16, CELLS), BF16),
-        in_specs=[SMEM] + [VMEM] * 3,
-        out_specs=VMEM,
-        compiler_params=PARAMS,
-        cost_estimate=cost(400_000_000, 4_000_000),
-        name="bubble",
-    )(index, spread, tiled, tile)
     phonon_part = pl.pallas_call(
         overlap_kernel,
         out_shape=jax.ShapeDtypeStruct((nx * nz, 4, 128), F32),

time: 88 us -> 89.7 us (1.019)
  waiting for transfers between devices: 22.9 us -> 26.5 us
  local copies, waits for them, and re-layouts: 6.03 us -> 4.29 us
    ppermute x1, waiting for transfers between devices: 0.44 us -> 3.36 us  [shards(): lax.ppermute(above, GRID, links(nx, nz, na, lambda c, h, a: (c - 1, h, a)))]
    all_to_all x1, local copies, waits for them, and re-layouts: 1.33 us -> 0.29 us  [shards(): lax.all_to_all(windows, ('h', 'atom'), split_axis=0, concat_axis=0, tiled...]
  transfers between devices with their start and end apart: 5 -> 5, of which waited for: 4 -> 4; matrix products, arithmetic and copies ran while one was open for 4% -> 4% of each run, Pallas kernels for 16% -> 12%
where the time goes in v2:
time: 89.7 us; the launch traced here: 89.2 us
  starting transfers between devices  39.9 us (44%)
  waiting for transfers between devices  26.5 us (30%)
  Pallas kernels  16.9 us (19%)
  local copies, waits for them, and re-layouts  4.29 us (5%)
    all_to_all x1, starting transfers between devices, shards(): lax.all_to_all(phonon_part, ('x', 'z'), split_axis=0, concat_axis=0, tile...  15.7 us
    all_to_all x1, starting transfers between devices, shards(): lax.all_to_all(windows, ('h', 'atom'), split_axis=0, concat_axis=0, tiled...  14 us
    all_to_all x1, waiting for transfers between devices, shards(): lax.all_to_all(windows, ('h', 'atom'), split_axis=0, concat_axis=0, tiled...  13 us
    all_to_all x1, starting transfers between devices, shards(): lax.all_to_all(message, ('h', 'atom'), split_axis=0, concat_axis=0, tiled...  7.66 us
    all_to_all x1, waiting for transfers between devices, shards(): lax.all_to_all(message, ('h', 'atom'), split_axis=0, concat_axis=0, tiled...  7.08 us
    pallas_call x1, Pallas kernels, shards(): pl.pallas_call(energy_kernel, out_shape=jax.ShapeDtypeStruct((16, 16, CEL...  5.61 us
    pallas_call x1, Pallas kernels, shards(): pl.pallas_call(spread_kernel, out_shape=(jax.ShapeDtypeStruct((16, NB, NO...  4.19 us
    ppermute x1, waiting for transfers between devices, shards(): lax.ppermute(above, GRID, links(nx, nz, na, lambda c, h, a: (c - 1, h, a)))  3.36 us
  transfers between devices with their start and end apart: 5, of which 4 were waited for; matrix products, arithmetic and copies ran while one was open for 4% of the time, Pallas kernels for 12%

profile of v2, /device:TPU:1, one launch (start us, length us, event | category | flops | bytes accessed | tf_op | source)
XLA Modules:
  0.0 89.2 jit_solution(8004356599235562569)
XLA Ops:
  0.6 0.9 %copy-done = bf16[2,1,128,256]{3,2,1,0:T(8,128)(2,1)S(1)} copy-done((bf16[2,1,128,256]{3,2,1,0:T(8,128)(2,1)S(1)}, bf16[2,1,128,256]{3,2,1,0:T(8,128)(2,1)}, u32[]{:S(2)}) %copy-start) | copy-done | bytes 131096
  1.5 0.8 shard_map.85
  2.4 14.0 %all-to-all-start = ((bf16[16,2,32,256]{3,2,1,0:T(8,128)(2,1)}), bf16[16,2,32,256]{3,2,1,0:T(8,128)(2,1)S(1)}, u32[]{:S(2)}, u32[]{:S(2)}) async-start(bf16[16,2,32,256]{3,2,1,0:T(8,128)(2,1)} %shard_map.85), calls=%async_computation | async-start | bytes 1048576 | tf_op jit(solution)/shard_map/all_to_all | solution.py:260
  16.4 0.1 copy.17.neighbours
  16.4 4.2 %shard_map.86 = (bf16[16,8,16,256]{3,2,1,0:T(8,128)(2,1)S(1)}, bf16[16,8,16,128]{3,2,1,0:T(8,128)(2,1)S(1)}, s32[128]{0:T(128)S(1)}) custom-call(s32[16,8]{1,0:T(8,128)S(1)} %copy.17.neighbours, bf16[16,8,256]{2,1,0:T(8,128)(2,1)S(1)} %copy-done.3), custom_call_target="tpu_custom_call" | custom-call | flops 500000000 | bytes 3000000 | tf_op jit(solution)/shard_map/pallas_call | solution.py:261
  20.6 13.0 %all-to-all-done = bf16[16,2,32,256]{3,2,1,0:T(8,128)(2,1)S(1)} async-done(((bf16[16,2,32,256]{3,2,1,0:T(8,128)(2,1)}), bf16[16,2,32,256]{3,2,1,0:T(8,128)(2,1)S(1)}, u32[]{:S(2)}, u32[]{:S(2)}) %all-to-all-start) | async-done | bytes 524320 | tf_op jit(solution)/shard_map/all_to_all | solution.py:260
  33.7 0.3 copy.28
  34.0 2.9 %bubble.1 = (bf16[8,128,256]{2,1,0:T(8,128)(2,1)S(1)}, bf16[32,16,256]{2,1,0:T(8,128)(2,1)S(1)}) custom-call(s32[128]{0:T(128)S(1)} %get-tuple-element.19.index, bf16[16,8,16,256]{3,2,1,0:T(8,128)(2,1)S(1)} %get-tuple-element.20.spread, bf16[16,8,16,128]{3,2,1,0:T(8,128)(2,1)S(1)} %get-tuple-element.21.tiled, bf16[2,32,16,256]{3,2,1,0:T(8,128)(2,1)S(1)} %bitcast.32), custom_call_target="tpu_custom_call" | custom-call | flops 400000000 | bytes 4000000 | tf_op jit(solution)/shard_map/bubble/pallas_call | solution.py:233
  36.9 1.3 %collective-permute-start = (bf16[32,16,256]{2,1,0:T(8,128)(2,1)S(1)}, bf16[32,16,256]{2,1,0:T(8,128)(2,1)S(1)}, u32[]{:S(2)}, u32[]{:S(2)}) collective-permute-start(bf16[32,16,256]{2,1,0:T(8,128)(2,1)S(1)} %get-tuple-element.23), channel_id=1, source_target_pairs={{0,16},{1,17},{2,18},{3,19},{4,20},{5,21},{6,22},{7,23},{16,32},{1... | collective-permute-start | bytes 786440 | tf_op jit(solution)/shard_map/ppermute | solution.py:279
  38.3 1.3 %collective-permute-start.1 = (bf16[8,8,256]{2,1,0:T(8,128)(2,1)S(1)}, bf16[8,8,256]{2,1,0:T(8,128)(2,1)S(1)}, u32[]{:S(2)}, u32[]{:S(2)}) collective-permute-start(bf16[8,8,256]{2,1,0:T(8,128)(2,1)S(1)} %dynamic-slice_bitcast_fusion.1), channel_id=1, source_target_pairs={{16,0},{17,1},{18,2},{19,3},{20,4},{21,5},{22,6},{23,7},{24,8},{25... | collective-permute-start | bytes 98312 | tf_op jit(solution)/shard_map/ppermute | solution.py:277
  39.6 3.4 %collective-permute-done.1.upper = bf16[8,8,256]{2,1,0:T(8,128)(2,1)S(1)} collective-permute-done((bf16[8,8,256]{2,1,0:T(8,128)(2,1)S(1)}, bf16[8,8,256]{2,1,0:T(8,128)(2,1)S(1)}, u32[]{:S(2)}, u32[]{:S(2)}) %collective-permute-start.1) | collective-permute-done | bytes 32800 | tf_op jit(solution)/shard_map/ppermute | solution.py:277
  42.9 1.2 %overlap.1 = f32[48,4,128]{2,1,0:T(4,128)} custom-call(bf16[8,128,256]{2,1,0:T(8,128)(2,1)S(1)} %get-tuple-element.24.bubble, bf16[2,32,16,256]{3,2,1,0:T(8,128)(2,1)S(1)} %bitcast.34, bf16[8,8,256]{2,1,0:T(8,128)(2,1)S(1)} %collective-permute-done.1.upper), custom_call_target="tpu_custom_call" | custom-call | flops 40000000 | bytes 1000000 | tf_op jit(solution)/shard_map/overlap/pallas_call | solution.py:280
  44.1 15.7 %all-to-all-start.1 = ((f32[48,4,128]{2,1,0:T(4,128)}), f32[48,4,128]{2,1,0:T(4,128)S(1)}, u32[]{:S(2)}, u32[]{:S(2)}) async-start(f32[48,4,128]{2,1,0:T(4,128)} %overlap.1), calls=%async_computation.1 | async-start | bytes 196608 | tf_op jit(solution)/shard_map/all_to_all | solution.py:290
  59.9 0.0 copy-start.2
  59.9 0.0 copy-start.4
  59.9 0.6 copy-done.1
  60.5 0.0 copy-done.2
  60.6 0.0 copy-done.4
  60.6 5.6 %energy.1 = bf16[16,16,256]{2,1,0:T(8,128)(2,1)S(1)} custom-call(s32[128]{0:T(128)S(1)} %get-tuple-element.19.index, s32[16]{0:T(128)S(1)} %copy-done.1, s32[16]{0:T(128)S(1)} %copy-done.2, f32[2,16]{1,0:T(2,128)S(1)} %copy-done.4, bf16[16,8,16,256]{3,2,1,0:T(8,128)(2,1)S(1)} %get-tuple-element.20.spread, ...), custom_call_target="tpu_custom_call" | custom-call | flops 800000000 | bytes 4000000 | tf_op jit(solution)/shard_map/energy/pallas_call | solution.py:294
  66.2 0.4 squeeze.15
  66.6 0.4 squeeze.16
  67.0 0.4 convolution_bitcast_fusion
  67.4 0.4 squeeze.13
  67.8 0.4 squeeze.14
  68.2 0.4 fusion
  68.6 0.1 reshape.23.current
  68.7 3.0 %all-to-all-done.1.parts = f32[48,4,128]{2,1,0:T(4,128)S(1)} async-done(((f32[48,4,128]{2,1,0:T(4,128)}), f32[48,4,128]{2,1,0:T(4,128)S(1)}, u32[]{:S(2)}, u32[]{:S(2)}) %all-to-all-start.1) | async-done | bytes 98336 | tf_op jit(solution)/shard_map/all_to_all | solution.py:290
  71.7 0.7 combine.1
  72.4 7.7 %all-to-all-start.2 = ((f32[16,8,128]{2,1,0:T(8,128)}), f32[16,8,128]{2,1,0:T(8,128)S(1)}, u32[]{:S(2)}, u32[]{:S(2)}) async-start(f32[16,8,128]{2,1,0:T(8,128)} %combine.1), calls=%async_computation.2 | async-start | bytes 131072 | tf_op jit(solution)/shard_map/all_to_all | solution.py:314
  80.1 0.7 copy.22
  80.8 7.1 %all-to-all-done.2.refs_2_ = f32[16,8,128]{2,1,0:T(8,128)S(1)} async-done(((f32[16,8,128]{2,1,0:T(8,128)}), f32[16,8,128]{2,1,0:T(8,128)S(1)}, u32[]{:S(2)}, u32[]{:S(2)}) %all-to-all-start.2) | async-done | bytes 65568 | tf_op jit(solution)/shard_map/all_to_all | solution.py:314
  87.8 1.4 %final.1 = (f32[16,128]{1,0:T(8,128)}, f32[1,256]{1,0:T(1,128)}) custom-call(s32[16]{0:T(128)S(1)} %copy-done.1, s32[16]{0:T(128)S(1)} %copy-done.2, f32[16,8,128]{2,1,0:T(8,128)S(1)} %all-to-all-done.2.refs_2_), custom_call_target="tpu_custom_call" | custom-call | tf_op jit(solution)/shard_map/final/pallas_call | solution.py:315
  (13 shorter events, 0.1 us)
Async XLA Ops:
  0.6 0.9 %copy-start = (bf16[2,1,128,256]{3,2,1,0:T(8,128)(2,1)S(1)}, bf16[2,1,128,256]{3,2,1,0:T(8,128)(2,1)}, u32[]{:S(2)}) copy-start(bf16[2,1,128,256]{3,2,1,0:T(8,128)(2,1)} %greens.1) | copy-start | bytes 393220
  2.4 14.0 %copy-start.5 = (s32[16,8]{0,1:T(8,128)S(1)}, s32[16,8]{0,1:T(8,128)}, u32[]{:S(2)}) copy-start(s32[16,8]{0,1:T(8,128)} %param.8) | copy-start | bytes 1540
  2.4 14.0 %copy-start.3 = (bf16[16,8,256]{2,1,0:T(8,128)(2,1)S(1)}, bf16[16,8,256]{2,1,0:T(8,128)(2,1)}, u32[]{:S(2)}) copy-start(bf16[16,8,256]{2,1,0:T(8,128)(2,1)} %coupling.1) | copy-start | bytes 196612
  2.4 31.3 %all-to-all-start = ((bf16[16,2,32,256]{3,2,1,0:T(8,128)(2,1)}), bf16[16,2,32,256]{3,2,1,0:T(8,128)(2,1)S(1)}, u32[]{:S(2)}, u32[]{:S(2)}) async-start(bf16[16,2,32,256]{3,2,1,0:T(8,128)(2,1)} %shard_map.85), calls=%async_computation | async-start | bytes 1048576 | tf_op jit(solution)/shard_map/all_to_all | solution.py:260
  36.9 22.9 %collective-permute-start = (bf16[32,16,256]{2,1,0:T(8,128)(2,1)S(1)}, bf16[32,16,256]{2,1,0:T(8,128)(2,1)S(1)}, u32[]{:S(2)}, u32[]{:S(2)}) collective-permute-start(bf16[32,16,256]{2,1,0:T(8,128)(2,1)S(1)} %get-tuple-element.23), channel_id=1, source_target_pairs={{0,16},{1,17},{2,18},{3,19},{4,20},{5,21},{6,22},{7,23},{16,32},{1... | collective-permute-start | bytes 786440 | tf_op jit(solution)/shard_map/ppermute | solution.py:279
  38.3 4.7 %collective-permute-start.1 = (bf16[8,8,256]{2,1,0:T(8,128)(2,1)S(1)}, bf16[8,8,256]{2,1,0:T(8,128)(2,1)S(1)}, u32[]{:S(2)}, u32[]{:S(2)}) collective-permute-start(bf16[8,8,256]{2,1,0:T(8,128)(2,1)S(1)} %dynamic-slice_bitcast_fusion.1), channel_id=1, source_target_pairs={{16,0},{17,1},{18,2},{19,3},{20,4},{21,5},{22,6},{23,7},{24,8},{25... | collective-permute-start | bytes 98312 | tf_op jit(solution)/shard_map/ppermute | solution.py:277
  44.1 27.6 %all-to-all-start.1 = ((f32[48,4,128]{2,1,0:T(4,128)}), f32[48,4,128]{2,1,0:T(4,128)S(1)}, u32[]{:S(2)}, u32[]{:S(2)}) async-start(f32[48,4,128]{2,1,0:T(4,128)} %overlap.1), calls=%async_computation.1 | async-start | bytes 196608 | tf_op jit(solution)/shard_map/all_to_all | solution.py:290
  59.9 0.7 copy-start.1
  59.9 0.7 copy-start.2
  59.9 0.7 copy-start.4
  72.4 15.4 %all-to-all-start.2 = ((f32[16,8,128]{2,1,0:T(8,128)}), f32[16,8,128]{2,1,0:T(8,128)S(1)}, u32[]{:S(2)}, u32[]{:S(2)}) async-start(f32[16,8,128]{2,1,0:T(8,128)} %combine.1), calls=%async_computation.2 | async-start | bytes 131072 | tf_op jit(solution)/shard_map/all_to_all | solution.py:314

commit v3 on v2

--- a/solution.py
+++ b/solution.py
@@ -45,7 +45,7 @@
                     out[d, field] = greens[field, 0, begin:end]
 
 
-def spread_kernel(neighbours, coupling, spread, tiled, index):
+def prepare_kernel(scale, neighbours, counts, offsets, coupling, spread, tiled, index, picks, live):
     row, col = iota((CELLS, CELLS), 0), iota((CELLS, CELLS), 1)
     pick_spread = (row // NO == col // NO).astype(F32).astype(BF16)
     pick_tiled = (row // NO == col % NO).astype(F32).astype(BF16)[:, 0:128]
@@ -54,6 +54,16 @@
     for a in range(coupling.shape[0]):
         for n in range(NB):
             index[a * NB + n] = neighbours[a, n] + shift
+    line = iota((8, 256), 1) % 128
+    wanted = jnp.zeros((8, 256), jnp.int32)
+    for w in range(NW):
+        wanted = jnp.where(line % NW == w, offsets[w], wanted)
+    source_row = iota((8, 256), 1) // 128 * 64 + line // NW * REACH + wanted - 1
+    picks[...] = (iota((128, 256), 0) == source_row[0:1]).astype(F32).astype(BF16)
+    used = jnp.zeros((16, NB * NW), jnp.int32)
+    for a in range(16):
+        used = jnp.where(iota((16, NB * NW), 0) == a, counts[a], used)
+    live[...] = jnp.where(iota((16, NB * NW), 1) // NW < used, scale, 0.0)
 
     def atom(a, carry):
         block = coupling[a].astype(F32)
@@ -68,15 +78,33 @@
     lax.fori_loop(0, coupling.shape[0], atom, 0)
 
 
+def exact_select(values, picks):
+    high = values.astype(BF16)
+    rest = values - high.astype(F32)
+    middle = rest.astype(BF16)
+    low = (rest - middle.astype(F32)).astype(BF16)
+    count = values.shape[0]
+    stacked = jnp.concatenate([high, middle, low], axis=0)
+    chosen = jnp.dot(stacked, picks, preferred_element_type=F32)
+    return chosen[0:count] + (chosen[count : 2 * count] + chosen[2 * count : 3 * count])
+
+
 def kron_rows(spread, tiled):
     tiled = jnp.concatenate([tiled, tiled], axis=1)
     product = spread.astype(F32)[:, None, :] * tiled.astype(F32)[None, :, :]
     return product.reshape(CELLS, CELLS).astype(BF16)
 
 
-def bubble_kernel(index, spread, tiled, tile, out, edge):
+def bubble_kernel(index_at, spread, tiled, tile, out, edge, index, arrived):
     half = lax.axis_index("h")
     first = half * 8
+    load = pltpu.make_async_copy(index_at, index, arrived)
+    load.start()
+    for b in range(tile.shape[1]):
+        for field in range(2):
+            kept = jnp.where(half == 0, tile[field, b, 8:16], tile[field, b, 0:8])
+            edge[b, field * 8 : field * 8 + 8] = kept
+    load.wait()
 
     def atom(a, carry):
         for n in range(NB):
@@ -87,10 +115,6 @@
         return carry
 
     lax.fori_loop(0, 8, atom, 0)
-    for b in range(tile.shape[1]):
-        for field in range(2):
-            kept = jnp.where(half == 0, tile[field, b, 8:16], tile[field, b, 0:8])
-            edge[b, field * 8 : field * 8 + 8] = kept
 
 
 def overlap_kernel(bubble, tile, upper, out, frame, terms):
@@ -108,63 +132,48 @@
             parts.append(jnp.sum(jnp.where(distance == d, overlap, 0.0), axis=0, keepdims=True))
         terms[a] = jnp.concatenate(parts, axis=0)
     column = iota((NB * 16, NB * REACH), 1)
-    gather = (iota((NB * 16, NB * REACH), 0) // 16 == column // REACH).astype(F32)
-    sums = jnp.dot(
-        terms[...].reshape(8 * REACH, NB * 16),
-        gather,
-        preferred_element_type=F32,
-        precision=lax.Precision.HIGHEST,
-    ).reshape(8, REACH, NB * REACH)
+    gather = iota((NB * 16, NB * REACH), 0) // 16 == column // REACH
+    gather = gather.astype(F32).astype(BF16)
+    sums = exact_select(terms[...].reshape(8 * REACH, NB * 16), gather)
+    sums = sums.reshape(8, REACH, NB * REACH)
     same = iota((REACH, NB * REACH), 0) == iota((REACH, NB * REACH), 1) % REACH
     total = jnp.sum(jnp.where(same[None], sums, 0.0), axis=1)
-    total = jnp.concatenate([total[0:4], total[4:8]], axis=1)
+    total = jnp.concatenate([total[0:4], total[4:8]], axis=1).astype(BF16)
     for copy in range(out.shape[0]):
         out[copy] = total
 
 
 def combine_kernel(parts, current, out):
     half = lax.axis_index("h")
-    total = parts[0]
+    total = parts[0].astype(F32)
     for column in range(1, parts.shape[0]):
-        total = total + parts[column]
+        total = total + parts[column].astype(F32)
     owners = current.shape[0]
     for h in range(2):
         mine = (half == h).astype(F32)
         for a in range(owners):
             d = h * owners + a
-            out[d, 0:1] = current[a : a + 1, 0:128] * mine
-            out[d, 1:2] = current[a : a + 1, 128:256] * mine
-            out[d, 2:6] = total
-            out[d, 6:8] = jnp.zeros((2, 128), F32)
-
-
-def final_kernel(scale_phonon, scale_current, counts, offsets, received, phonon, current):
+            out[d, 0, 0:1] = current[a : a + 1, 0:128] * mine
+            out[d, 0, 1:2] = current[a : a + 1, 128:256] * mine
+            out[d, 1] = total[0:2]
+            out[d, 2] = total[2:4]
+
+
+def final_kernel(scale, received, picks, live, phonon, current):
     atom = lax.axis_index("atom")
-    owners = received.shape[0] // 2
-    total = received[0]
+    other = received.shape[0] // 2 + atom
+    total = received[0, 0]
     for source in range(1, received.shape[0]):
-        total = total + received[source]
-    current[0:1, 0:128] = total[0:1] * scale_current
-    current[0:1, 128:256] = total[1:2] * scale_current
-    sums = jnp.concatenate([received[atom, 2:6], received[owners + atom, 2:6]], axis=0)
-    row, col = iota((128, 128), 0), iota((128, 128), 1)
-    wanted = jnp.zeros((128, 128), jnp.int32)
-    for w in range(NW):
-        wanted = jnp.where(col % NW == w, offsets[w], wanted)
-    slot = (row % 64) // REACH == col // NW
-    match = slot & (row % REACH + 1 == wanted)
-    pieces = []
-    for side in range(2):
-        expand = (match & (row // 64 == side)).astype(F32)
-        pieces.append(
-            jnp.dot(sums, expand, preferred_element_type=F32, precision=lax.Precision.HIGHEST)
-        )
-    values = jnp.concatenate([pieces[0][0:4], pieces[1][0:4], pieces[0][4:8], pieces[1][4:8]], axis=0)
-    live = jnp.zeros((16, NB * NW), jnp.int32)
-    line = iota((16, NB * NW), 0)
-    for a in range(16):
-        live = jnp.where(line == a, counts[a], live)
-    phonon[...] = jnp.where(iota((16, NB * NW), 1) // NW < live, values * scale_phonon, 0.0)
+        total = total + received[source, 0]
+    current[0:1, 0:128] = total[0:1] * scale
+    current[0:1, 128:256] = total[1:2] * scale
+    sums = jnp.concatenate(
+        [received[atom, 1], received[atom, 2], received[other, 1], received[other, 2]], axis=0
+    )
+    values = exact_select(sums, picks[...])
+    near, far = values[:, 0:128], values[:, 128:256]
+    values = jnp.concatenate([near[0:4], far[0:4], near[4:8], far[4:8]], axis=0)
+    phonon[...] = values * live[...]
 
 
 def mix_table(phonon_weights, offsets, half):
@@ -236,8 +245,9 @@
             jax.ShapeDtypeStruct((8, NB * 16, CELLS), BF16),
             jax.ShapeDtypeStruct((32, 16, CELLS), BF16),
         ),
-        in_specs=[SMEM] + [VMEM] * 3,
+        in_specs=[pl.BlockSpec(memory_space=pl.ANY)] + [VMEM] * 3,
         out_specs=(VMEM, VMEM),
+        scratch_shapes=[pltpu.SMEM((16 * NB,), jnp.int32), pltpu.SemaphoreType.DMA],
         compiler_params=PARAMS,
         cost_estimate=cost(400_000_000, 4_000_000),
         name="bubble",
@@ -258,18 +268,20 @@
         cost_estimate=cost(1000, 700_000),
     )(greens)
     received = lax.all_to_all(windows, ("h", "atom"), split_axis=0, concat_axis=0, tiled=True)
-    spread, tiled, index = pl.pallas_call(
-        spread_kernel,
+    spread, tiled, index, picks, live = pl.pallas_call(
+        lambda *refs: prepare_kernel(scale_phonon, *refs),
         out_shape=(
             jax.ShapeDtypeStruct((16, NB, NO, CELLS), BF16),
             jax.ShapeDtypeStruct((16, NB, NO, 128), BF16),
             jax.ShapeDtypeStruct((16 * NB,), jnp.int32),
+            jax.ShapeDtypeStruct((128, 256), BF16),
+            jax.ShapeDtypeStruct((16, NB * NW), F32),
         ),
-        in_specs=[SMEM, VMEM],
-        out_specs=(VMEM, VMEM, SMEM),
+        in_specs=[SMEM, SMEM, SMEM, VMEM],
+        out_specs=(VMEM, VMEM, SMEM, VMEM, VMEM),
         compiler_params=PARAMS,
         cost_estimate=cost(500_000_000, 3_000_000),
-    )(neighbours, coupling)
+    )(neighbours, counts, offsets, coupling)
 
     tile = jnp.transpose(received, (1, 2, 0, 3))
     tile, spread, tiled, index = lax.optimization_barrier((tile, spread, tiled, index))
@@ -279,7 +291,7 @@
     ring = lax.ppermute(edge, GRID, links(nx, nz, na, lambda c, h, a: (c + 1 - 2 * h, h, a)))
     phonon_part = pl.pallas_call(
         overlap_kernel,
-        out_shape=jax.ShapeDtypeStruct((nx * nz, 4, 128), F32),
+        out_shape=jax.ShapeDtypeStruct((nx * nz, 4, 128), BF16),
         in_specs=[VMEM] * 3,
         out_specs=VMEM,
         scratch_shapes=[pltpu.VMEM((8, 32, CELLS), BF16), pltpu.VMEM((8, REACH, NB * 16), F32)],
@@ -305,7 +317,7 @@
     current_part = collision(self_energy, own)
     message = pl.pallas_call(
         combine_kernel,
-        out_shape=jax.ShapeDtypeStruct((2 * na, 8, 128), F32),
+        out_shape=jax.ShapeDtypeStruct((2 * na, 3, 2, 128), F32),
         in_specs=[VMEM, VMEM],
         out_specs=VMEM,
         compiler_params=PARAMS,
@@ -313,16 +325,16 @@
     )(parts, current_part)
     received_sums = lax.all_to_all(message, ("h", "atom"), split_axis=0, concat_axis=0, tiled=True)
     phonon_self, current = pl.pallas_call(
-        lambda *refs: final_kernel(scale_phonon, scale_current, *refs),
+        lambda *refs: final_kernel(scale_current, *refs),
         out_shape=(
             jax.ShapeDtypeStruct((16, NB * NW), F32),
             jax.ShapeDtypeStruct((1, CELLS), F32),
         ),
-        in_specs=[SMEM, SMEM, VMEM],
+        in_specs=[VMEM] * 3,
         out_specs=(VMEM, VMEM),
         compiler_params=PARAMS,
         name="final",
-    )(counts, offsets, received_sums)
+    )(received_sums, picks, live)
     return (self_energy, phonon_self, current)
 
 

time: 89.7 us -> 88.1 us (0.982)
  waiting for transfers between devices: 26.5 us -> 25.1 us
  transfers between devices with their start and end apart: 5 -> 5, of which waited for: 4 -> 4; matrix products, arithmetic and copies ran while one was open for 4% -> 4% of each run, Pallas kernels for 12% -> 13%
where the time goes in v3:
time: 88.1 us; the launch traced here: 87.6 us
  starting transfers between devices  39.8 us (45%)
  waiting for transfers between devices  25.1 us (28%)
  Pallas kernels  16.2 us (18%)
  local copies, waits for them, and re-layouts  4.84 us (5%)
    all_to_all x1, starting transfers between devices, shards(): lax.all_to_all(phonon_part, ('x', 'z'), split_axis=0, concat_axis=0, tile...  15.7 us
    all_to_all x1, starting transfers between devices, shards(): lax.all_to_all(windows, ('h', 'atom'), split_axis=0, concat_axis=0, tiled...  14 us
    all_to_all x1, waiting for transfers between devices, shards(): lax.all_to_all(windows, ('h', 'atom'), split_axis=0, concat_axis=0, tiled...  12.4 us
    all_to_all x1, starting transfers between devices, shards(): lax.all_to_all(message, ('h', 'atom'), split_axis=0, concat_axis=0, tiled...  7.59 us
    all_to_all x1, waiting for transfers between devices, shards(): lax.all_to_all(message, ('h', 'atom'), split_axis=0, concat_axis=0, tiled...  6.78 us
    pallas_call x1, Pallas kernels, shards(): pl.pallas_call(energy_kernel, out_shape=jax.ShapeDtypeStruct((16, 16, CEL...  5.63 us
    pallas_call x1, Pallas kernels, shards(): pl.pallas_call(lambda *refs: prepare_kernel(scale_phonon, *refs), out_sha...  4.23 us
    ppermute x1, waiting for transfers between devices, shards(): lax.ppermute(above, GRID, links(nx, nz, na, lambda c, h, a: (c - 1, h, a)))  3.36 us
  transfers between devices with their start and end apart: 5, of which 4 were waited for; matrix products, arithmetic and copies ran while one was open for 4% of the time, Pallas kernels for 13%

profile of v3, /device:TPU:1, one launch (start us, length us, event | category | flops | bytes accessed | tf_op | source)
XLA Modules:
  0.0 87.6 jit_solution(9912558515720098324)
XLA Ops:
  0.6 0.9 %copy-done = bf16[2,1,128,256]{3,2,1,0:T(8,128)(2,1)S(1)} copy-done((bf16[2,1,128,256]{3,2,1,0:T(8,128)(2,1)S(1)}, bf16[2,1,128,256]{3,2,1,0:T(8,128)(2,1)}, u32[]{:S(2)}) %copy-start) | copy-done | bytes 131096
  1.5 0.8 shard_map.85
  2.4 14.0 %all-to-all-start = ((bf16[16,2,32,256]{3,2,1,0:T(8,128)(2,1)}), bf16[16,2,32,256]{3,2,1,0:T(8,128)(2,1)S(1)}, u32[]{:S(2)}, u32[]{:S(2)}) async-start(bf16[16,2,32,256]{3,2,1,0:T(8,128)(2,1)} %shard_map.85), calls=%async_computation | async-start | bytes 1048576 | tf_op jit(solution)/shard_map/all_to_all | solution.py:270
  16.4 0.0 copy-start.3
  16.4 0.0 copy-start.4
  16.4 0.1 copy.17.refs_0_
  16.5 0.6 copy-done.3
  17.0 0.0 copy-done.4
  17.0 4.2 %shard_map.86 = (bf16[16,8,16,256]{3,2,1,0:T(8,128)(2,1)S(1)}, bf16[16,8,16,128]{3,2,1,0:T(8,128)(2,1)S(1)}, s32[128]{0:T(128)S(1)}, bf16[128,256]{1,0:T(8,128)(2,1)S(1)}, f32[16,128]{1,0:T(8,128)S(1)}) custom-call(s32[16,8]{1,0:T(8,128)S(1)} %copy.17.refs_0_, s32[16]{0:T(128)S(1)} %copy-done.3, s32[16]{0:T(128)S(1)} %copy-done.4, ...), custom_call_target="tpu_custom_call" | custom-call | flops 500000000 | bytes 3000000 | tf_op jit(solution)/shard_map/pallas_call | solution.py:271
  21.3 12.4 %all-to-all-done = bf16[16,2,32,256]{3,2,1,0:T(8,128)(2,1)S(1)} async-done(((bf16[16,2,32,256]{3,2,1,0:T(8,128)(2,1)}), bf16[16,2,32,256]{3,2,1,0:T(8,128)(2,1)S(1)}, u32[]{:S(2)}, u32[]{:S(2)}) %all-to-all-start) | async-done | bytes 524320 | tf_op jit(solution)/shard_map/all_to_all | solution.py:270
  33.7 0.3 copy.28
  34.0 2.9 %bubble.1 = (bf16[8,128,256]{2,1,0:T(8,128)(2,1)S(1)}, bf16[32,16,256]{2,1,0:T(8,128)(2,1)S(1)}) custom-call(s32[128]{0:T(128)S(1)} %get-tuple-element.21.index_at.index, bf16[16,8,16,256]{3,2,1,0:T(8,128)(2,1)S(1)} %get-tuple-element.22.spread, bf16[16,8,16,128]{3,2,1,0:T(8,128)(2,1)S(1)} %get-tuple-element.23.tiled, bf16[2,32,16,256]{3,2,1,0:T(8,128)(2,1)S(1)} %bitcast.32), custom_call_target="tpu_custom_call" | custom-call | flops 400000000 | bytes 4000000 | tf_op jit(solution)/shard_map/bubble/pallas_call | solution.py:242
  36.9 1.3 %collective-permute-start = (bf16[32,16,256]{2,1,0:T(8,128)(2,1)S(1)}, bf16[32,16,256]{2,1,0:T(8,128)(2,1)S(1)}, u32[]{:S(2)}, u32[]{:S(2)}) collective-permute-start(bf16[32,16,256]{2,1,0:T(8,128)(2,1)S(1)} %get-tuple-element.25), channel_id=1, source_target_pairs={{0,16},{1,17},{2,18},{3,19},{4,20},{5,21},{6,22},{7,23},{16,32},{1... | collective-permute-start | bytes 786440 | tf_op jit(solution)/shard_map/ppermute | solution.py:291
  38.2 1.3 %collective-permute-start.1 = (bf16[8,8,256]{2,1,0:T(8,128)(2,1)S(1)}, bf16[8,8,256]{2,1,0:T(8,128)(2,1)S(1)}, u32[]{:S(2)}, u32[]{:S(2)}) collective-permute-start(bf16[8,8,256]{2,1,0:T(8,128)(2,1)S(1)} %dynamic-slice_bitcast_fusion.1), channel_id=1, source_target_pairs={{16,0},{17,1},{18,2},{19,3},{20,4},{21,5},{22,6},{23,7},{24,8},{25... | collective-permute-start | bytes 98312 | tf_op jit(solution)/shard_map/ppermute | solution.py:289
  39.5 3.4 %collective-permute-done.1.upper = bf16[8,8,256]{2,1,0:T(8,128)(2,1)S(1)} collective-permute-done((bf16[8,8,256]{2,1,0:T(8,128)(2,1)S(1)}, bf16[8,8,256]{2,1,0:T(8,128)(2,1)S(1)}, u32[]{:S(2)}, u32[]{:S(2)}) %collective-permute-start.1) | collective-permute-done | bytes 32800 | tf_op jit(solution)/shard_map/ppermute | solution.py:289
  42.9 1.2 %overlap.1 = bf16[48,4,128]{2,1,0:T(4,128)(2,1)} custom-call(bf16[8,128,256]{2,1,0:T(8,128)(2,1)S(1)} %get-tuple-element.26.bubble, bf16[2,32,16,256]{3,2,1,0:T(8,128)(2,1)S(1)} %bitcast.34, bf16[8,8,256]{2,1,0:T(8,128)(2,1)S(1)} %collective-permute-done.1.upper), custom_call_target="tpu_custom_call" | custom-call | flops 40000000 | bytes 1000000 | tf_op jit(solution)/shard_map/overlap/pallas_call | solution.py:292
  44.1 15.7 %all-to-all-start.1 = ((bf16[48,4,128]{2,1,0:T(4,128)(2,1)}), bf16[48,4,128]{2,1,0:T(4,128)(2,1)S(1)}, u32[]{:S(2)}, u32[]{:S(2)}) async-start(bf16[48,4,128]{2,1,0:T(4,128)(2,1)} %overlap.1), calls=%async_computation.1 | async-start | bytes 98304 | tf_op jit(solution)/shard_map/all_to_all | solution.py:302
  59.8 0.7 copy-done.2
  60.5 5.6 %energy.1 = bf16[16,16,256]{2,1,0:T(8,128)(2,1)S(1)} custom-call(s32[128]{0:T(128)S(1)} %get-tuple-element.21.index_at.index, s32[16]{0:T(128)S(1)} %copy-done.3, s32[16]{0:T(128)S(1)} %copy-done.4, f32[2,16]{1,0:T(2,128)S(1)} %copy-done.2, bf16[16,8,16,256]{3,2,1,0:T(8,128)(2,1)S(1)} %get-tuple-element.22.spread, ...), custom_call_target="tpu_custom_call" | custom-call | flops 800000000 | bytes 4000000 | tf_op jit(solution)/shard_map/energy/pallas_call | solution.py:306
  66.1 0.4 squeeze.13
  66.5 0.4 squeeze.14
  66.9 0.4 squeeze.15
  67.3 0.4 squeeze.16
  67.6 0.4 convolution_bitcast_fusion
  68.1 0.4 fusion
  68.5 0.1 reshape.23.current
  68.6 2.5 %all-to-all-done.1.parts = bf16[48,4,128]{2,1,0:T(4,128)(2,1)S(1)} async-done(((bf16[48,4,128]{2,1,0:T(4,128)(2,1)}), bf16[48,4,128]{2,1,0:T(4,128)(2,1)S(1)}, u32[]{:S(2)}, u32[]{:S(2)}) %all-to-all-start.1) | async-done | bytes 49184 | tf_op jit(solution)/shard_map/all_to_all | solution.py:302
  71.1 0.7 combine.1
  71.8 7.6 %all-to-all-start.2 = ((f32[16,3,2,128]{3,2,1,0:T(2,128)}), f32[16,3,2,128]{3,2,1,0:T(2,128)S(1)}, u32[]{:S(2)}, u32[]{:S(2)}) async-start(f32[16,3,2,128]{3,2,1,0:T(2,128)} %combine.1), calls=%async_computation.2 | async-start | bytes 98304 | tf_op jit(solution)/shard_map/all_to_all | solution.py:326
  79.4 0.7 copy.22
  80.1 6.8 %all-to-all-done.2.refs_0_ = f32[16,3,2,128]{3,2,1,0:T(2,128)S(1)} async-done(((f32[16,3,2,128]{3,2,1,0:T(2,128)}), f32[16,3,2,128]{3,2,1,0:T(2,128)S(1)}, u32[]{:S(2)}, u32[]{:S(2)}) %all-to-all-start.2) | async-done | bytes 49184 | tf_op jit(solution)/shard_map/all_to_all | solution.py:326
  86.9 0.7 final.1
  (13 shorter events, 0.1 us)
Async XLA Ops:
  0.6 0.9 %copy-start = (bf16[2,1,128,256]{3,2,1,0:T(8,128)(2,1)S(1)}, bf16[2,1,128,256]{3,2,1,0:T(8,128)(2,1)}, u32[]{:S(2)}) copy-start(bf16[2,1,128,256]{3,2,1,0:T(8,128)(2,1)} %greens.1) | copy-start | bytes 393220
  2.4 14.0 %copy-start.5 = (s32[16,8]{0,1:T(8,128)S(1)}, s32[16,8]{0,1:T(8,128)}, u32[]{:S(2)}) copy-start(s32[16,8]{0,1:T(8,128)} %param.8) | copy-start | bytes 1540
  2.4 14.1 %copy-start.1 = (bf16[16,8,256]{2,1,0:T(8,128)(2,1)S(1)}, bf16[16,8,256]{2,1,0:T(8,128)(2,1)}, u32[]{:S(2)}) copy-start(bf16[16,8,256]{2,1,0:T(8,128)(2,1)} %refs_3_.1) | copy-start | bytes 196612
  2.4 31.3 %all-to-all-start = ((bf16[16,2,32,256]{3,2,1,0:T(8,128)(2,1)}), bf16[16,2,32,256]{3,2,1,0:T(8,128)(2,1)S(1)}, u32[]{:S(2)}, u32[]{:S(2)}) async-start(bf16[16,2,32,256]{3,2,1,0:T(8,128)(2,1)} %shard_map.85), calls=%async_computation | async-start | bytes 1048576 | tf_op jit(solution)/shard_map/all_to_all | solution.py:270
  16.4 0.7 copy-start.3
  16.4 0.7 copy-start.4
  36.9 22.9 %collective-permute-start = (bf16[32,16,256]{2,1,0:T(8,128)(2,1)S(1)}, bf16[32,16,256]{2,1,0:T(8,128)(2,1)S(1)}, u32[]{:S(2)}, u32[]{:S(2)}) collective-permute-start(bf16[32,16,256]{2,1,0:T(8,128)(2,1)S(1)} %get-tuple-element.25), channel_id=1, source_target_pairs={{0,16},{1,17},{2,18},{3,19},{4,20},{5,21},{6,22},{7,23},{16,32},{1... | collective-permute-start | bytes 786440 | tf_op jit(solution)/shard_map/ppermute | solution.py:291
  38.2 4.7 %collective-permute-start.1 = (bf16[8,8,256]{2,1,0:T(8,128)(2,1)S(1)}, bf16[8,8,256]{2,1,0:T(8,128)(2,1)S(1)}, u32[]{:S(2)}, u32[]{:S(2)}) collective-permute-start(bf16[8,8,256]{2,1,0:T(8,128)(2,1)S(1)} %dynamic-slice_bitcast_fusion.1), channel_id=1, source_target_pairs={{16,0},{17,1},{18,2},{19,3},{20,4},{21,5},{22,6},{23,7},{24,8},{25... | collective-permute-start | bytes 98312 | tf_op jit(solution)/shard_map/ppermute | solution.py:289
  44.1 27.1 %all-to-all-start.1 = ((bf16[48,4,128]{2,1,0:T(4,128)(2,1)}), bf16[48,4,128]{2,1,0:T(4,128)(2,1)S(1)}, u32[]{:S(2)}, u32[]{:S(2)}) async-start(bf16[48,4,128]{2,1,0:T(4,128)(2,1)} %overlap.1), calls=%async_computation.1 | async-start | bytes 98304 | tf_op jit(solution)/shard_map/all_to_all | solution.py:302
  59.8 0.7 copy-start.2
  71.8 15.1 %all-to-all-start.2 = ((f32[16,3,2,128]{3,2,1,0:T(2,128)}), f32[16,3,2,128]{3,2,1,0:T(2,128)S(1)}, u32[]{:S(2)}, u32[]{:S(2)}) async-start(f32[16,3,2,128]{3,2,1,0:T(2,128)} %combine.1), calls=%async_computation.2 | async-start | bytes 98304 | tf_op jit(solution)/shard_map/all_to_all | solution.py:326

commit v4 on v3

--- a/solution.py
+++ b/solution.py
@@ -106,15 +106,12 @@
             edge[b, field * 8 : field * 8 + 8] = kept
     load.wait()
 
-    def atom(a, carry):
+    for a in range(out.shape[0]):
         for n in range(NB):
             matrix = kron_rows(spread[first + a, n], tiled[first + a, n])
             block = tile[1, index[(first + a) * NB + n]]
             product = jnp.dot(block, matrix, preferred_element_type=F32)
             out[a, n * 16 : n * 16 + 16] = product.astype(BF16)
-        return carry
-
-    lax.fori_loop(0, 8, atom, 0)
 
 
 def overlap_kernel(bubble, tile, upper, out, frame, terms):
@@ -198,7 +195,7 @@
         frame = jnp.concatenate([tile[0, a], tile[1, a], ring[a]], axis=0)
         mixed[a] = jnp.dot(table, frame, preferred_element_type=F32).astype(BF16)
 
-    def atom(a, carry):
+    for a in range(out.shape[0]):
         total = jnp.zeros((NO, CELLS), F32)
         for n in range(NB):
             matrix = kron_rows(spread[a, n], tiled[a, n])
@@ -206,9 +203,6 @@
             live = (n < counts[a]).astype(F32)
             total = total + live * jnp.dot(block, matrix, preferred_element_type=F32)
         out[a] = total.astype(BF16)
-        return carry
-
-    lax.fori_loop(0, out.shape[0], atom, 0)
 
 
 def links(nx, nz, na, target):

time: 88.1 us -> 87.2 us (0.990)
  Pallas kernels: 16.2 us -> 13.5 us
  waiting for transfers between devices: 25.1 us -> 26.9 us
    pallas_call x1, Pallas kernels: 5.63 us -> 3.8 us  [shards(): pl.pallas_call(energy_kernel, out_shape=jax.ShapeDtypeStruct((16, 16, CEL...]
    all_to_all x1, waiting for transfers between devices: 2.53 us -> 4.35 us  [shards(): lax.all_to_all(phonon_part, ('x', 'z'), split_axis=0, concat_axis=0, tile...]
  transfers between devices with their start and end apart: 5 -> 5, of which waited for: 4 -> 4; matrix products, arithmetic and copies ran while one was open for 4% -> 4% of each run, Pallas kernels for 13% -> 11%
where the time goes in v4:
time: 87.2 us; the launch traced here: 86.8 us
  starting transfers between devices  39.8 us (46%)
  waiting for transfers between devices  26.9 us (31%)
  Pallas kernels  13.5 us (15%)
  local copies, waits for them, and re-layouts  4.84 us (6%)
    all_to_all x1, starting transfers between devices, shards(): lax.all_to_all(phonon_part, ('x', 'z'), split_axis=0, concat_axis=0, tile...  15.7 us
    all_to_all x1, starting transfers between devices, shards(): lax.all_to_all(windows, ('h', 'atom'), split_axis=0, concat_axis=0, tiled...  14 us
    all_to_all x1, waiting for transfers between devices, shards(): lax.all_to_all(windows, ('h', 'atom'), split_axis=0, concat_axis=0, tiled...  12.4 us
    all_to_all x1, starting transfers between devices, shards(): lax.all_to_all(message, ('h', 'atom'), split_axis=0, concat_axis=0, tiled...  7.59 us
    all_to_all x1, waiting for transfers between devices, shards(): lax.all_to_all(message, ('h', 'atom'), split_axis=0, concat_axis=0, tiled...  6.78 us
    all_to_all x1, waiting for transfers between devices, shards(): lax.all_to_all(phonon_part, ('x', 'z'), split_axis=0, concat_axis=0, tile...  4.35 us
    pallas_call x1, Pallas kernels, shards(): pl.pallas_call(lambda *refs: prepare_kernel(scale_phonon, *refs), out_sha...  4.23 us
    pallas_call x1, Pallas kernels, shards(): pl.pallas_call(energy_kernel, out_shape=jax.ShapeDtypeStruct((16, 16, CEL...  3.8 us
  transfers between devices with their start and end apart: 5, of which 4 were waited for; matrix products, arithmetic and copies ran while one was open for 4% of the time, Pallas kernels for 11%

profile of v4, /device:TPU:1, one launch (start us, length us, event | category | flops | bytes accessed | tf_op | source)
XLA Modules:
  0.0 86.8 jit_solution(9650623854902906080)
XLA Ops:
  0.6 0.9 %copy-done = bf16[2,1,128,256]{3,2,1,0:T(8,128)(2,1)S(1)} copy-done((bf16[2,1,128,256]{3,2,1,0:T(8,128)(2,1)S(1)}, bf16[2,1,128,256]{3,2,1,0:T(8,128)(2,1)}, u32[]{:S(2)}) %copy-start) | copy-done | bytes 131096
  1.5 0.8 shard_map.85
  2.4 14.0 %all-to-all-start = ((bf16[16,2,32,256]{3,2,1,0:T(8,128)(2,1)}), bf16[16,2,32,256]{3,2,1,0:T(8,128)(2,1)S(1)}, u32[]{:S(2)}, u32[]{:S(2)}) async-start(bf16[16,2,32,256]{3,2,1,0:T(8,128)(2,1)} %shard_map.85), calls=%async_computation | async-start | bytes 1048576 | tf_op jit(solution)/shard_map/all_to_all | solution.py:264
  16.4 0.0 copy-start.3
  16.4 0.0 copy-start.4
  16.4 0.1 copy.17.refs_0_
  16.5 0.6 copy-done.3
  17.0 0.0 copy-done.4
  17.0 4.2 %shard_map.86 = (bf16[16,8,16,256]{3,2,1,0:T(8,128)(2,1)S(1)}, bf16[16,8,16,128]{3,2,1,0:T(8,128)(2,1)S(1)}, s32[128]{0:T(128)S(1)}, bf16[128,256]{1,0:T(8,128)(2,1)S(1)}, f32[16,128]{1,0:T(8,128)S(1)}) custom-call(s32[16,8]{1,0:T(8,128)S(1)} %copy.17.refs_0_, s32[16]{0:T(128)S(1)} %copy-done.3, s32[16]{0:T(128)S(1)} %copy-done.4, ...), custom_call_target="tpu_custom_call" | custom-call | flops 500000000 | bytes 3000000 | tf_op jit(solution)/shard_map/pallas_call | solution.py:265
  21.3 12.4 %all-to-all-done = bf16[16,2,32,256]{3,2,1,0:T(8,128)(2,1)S(1)} async-done(((bf16[16,2,32,256]{3,2,1,0:T(8,128)(2,1)}), bf16[16,2,32,256]{3,2,1,0:T(8,128)(2,1)S(1)}, u32[]{:S(2)}, u32[]{:S(2)}) %all-to-all-start) | async-done | bytes 524320 | tf_op jit(solution)/shard_map/all_to_all | solution.py:264
  33.7 0.3 copy.28
  34.0 2.1 %bubble.1 = (bf16[8,128,256]{2,1,0:T(8,128)(2,1)S(1)}, bf16[32,16,256]{2,1,0:T(8,128)(2,1)S(1)}) custom-call(s32[128]{0:T(128)S(1)} %get-tuple-element.21.index_at.index, bf16[16,8,16,256]{3,2,1,0:T(8,128)(2,1)S(1)} %get-tuple-element.22.spread, bf16[16,8,16,128]{3,2,1,0:T(8,128)(2,1)S(1)} %get-tuple-element.23.tiled, bf16[2,32,16,256]{3,2,1,0:T(8,128)(2,1)S(1)} %bitcast.32), custom_call_target="tpu_custom_call" | custom-call | flops 400000000 | bytes 4000000 | tf_op jit(solution)/shard_map/bubble/pallas_call | solution.py:236
  36.0 1.3 %collective-permute-start = (bf16[32,16,256]{2,1,0:T(8,128)(2,1)S(1)}, bf16[32,16,256]{2,1,0:T(8,128)(2,1)S(1)}, u32[]{:S(2)}, u32[]{:S(2)}) collective-permute-start(bf16[32,16,256]{2,1,0:T(8,128)(2,1)S(1)} %get-tuple-element.25), channel_id=1, source_target_pairs={{0,16},{1,17},{2,18},{3,19},{4,20},{5,21},{6,22},{7,23},{16,32},{1... | collective-permute-start | bytes 786440 | tf_op jit(solution)/shard_map/ppermute | solution.py:285
  37.4 1.3 %collective-permute-start.1 = (bf16[8,8,256]{2,1,0:T(8,128)(2,1)S(1)}, bf16[8,8,256]{2,1,0:T(8,128)(2,1)S(1)}, u32[]{:S(2)}, u32[]{:S(2)}) collective-permute-start(bf16[8,8,256]{2,1,0:T(8,128)(2,1)S(1)} %dynamic-slice_bitcast_fusion.1), channel_id=1, source_target_pairs={{16,0},{17,1},{18,2},{19,3},{20,4},{21,5},{22,6},{23,7},{24,8},{25... | collective-permute-start | bytes 98312 | tf_op jit(solution)/shard_map/ppermute | solution.py:283
  38.7 3.4 %collective-permute-done.1.upper = bf16[8,8,256]{2,1,0:T(8,128)(2,1)S(1)} collective-permute-done((bf16[8,8,256]{2,1,0:T(8,128)(2,1)S(1)}, bf16[8,8,256]{2,1,0:T(8,128)(2,1)S(1)}, u32[]{:S(2)}, u32[]{:S(2)}) %collective-permute-start.1) | collective-permute-done | bytes 32800 | tf_op jit(solution)/shard_map/ppermute | solution.py:283
  42.1 1.2 %overlap.1 = bf16[48,4,128]{2,1,0:T(4,128)(2,1)} custom-call(bf16[8,128,256]{2,1,0:T(8,128)(2,1)S(1)} %get-tuple-element.26.bubble, bf16[2,32,16,256]{3,2,1,0:T(8,128)(2,1)S(1)} %bitcast.34, bf16[8,8,256]{2,1,0:T(8,128)(2,1)S(1)} %collective-permute-done.1.upper), custom_call_target="tpu_custom_call" | custom-call | flops 40000000 | bytes 1000000 | tf_op jit(solution)/shard_map/overlap/pallas_call | solution.py:286
  43.2 15.7 %all-to-all-start.1 = ((bf16[48,4,128]{2,1,0:T(4,128)(2,1)}), bf16[48,4,128]{2,1,0:T(4,128)(2,1)S(1)}, u32[]{:S(2)}, u32[]{:S(2)}) async-start(bf16[48,4,128]{2,1,0:T(4,128)(2,1)} %overlap.1), calls=%async_computation.1 | async-start | bytes 98304 | tf_op jit(solution)/shard_map/all_to_all | solution.py:296
  59.0 0.7 copy-done.2
  59.6 3.8 %energy.1 = bf16[16,16,256]{2,1,0:T(8,128)(2,1)S(1)} custom-call(s32[128]{0:T(128)S(1)} %get-tuple-element.21.index_at.index, s32[16]{0:T(128)S(1)} %copy-done.3, s32[16]{0:T(128)S(1)} %copy-done.4, f32[2,16]{1,0:T(2,128)S(1)} %copy-done.2, bf16[16,8,16,256]{3,2,1,0:T(8,128)(2,1)S(1)} %get-tuple-element.22.spread, ...), custom_call_target="tpu_custom_call" | custom-call | flops 800000000 | bytes 4000000 | tf_op jit(solution)/shard_map/energy/pallas_call | solution.py:300
  63.5 0.4 squeeze.13
  63.8 0.4 squeeze.14
  64.2 0.4 squeeze.15
  64.6 0.4 squeeze.16
  65.0 0.4 convolution_bitcast_fusion
  65.4 0.4 fusion
  65.8 0.1 reshape.23.current
  65.9 4.4 %all-to-all-done.1.parts = bf16[48,4,128]{2,1,0:T(4,128)(2,1)S(1)} async-done(((bf16[48,4,128]{2,1,0:T(4,128)(2,1)}), bf16[48,4,128]{2,1,0:T(4,128)(2,1)S(1)}, u32[]{:S(2)}, u32[]{:S(2)}) %all-to-all-start.1) | async-done | bytes 49184 | tf_op jit(solution)/shard_map/all_to_all | solution.py:296
  70.3 0.7 combine.1
  71.0 7.6 %all-to-all-start.2 = ((f32[16,3,2,128]{3,2,1,0:T(2,128)}), f32[16,3,2,128]{3,2,1,0:T(2,128)S(1)}, u32[]{:S(2)}, u32[]{:S(2)}) async-start(f32[16,3,2,128]{3,2,1,0:T(2,128)} %combine.1), calls=%async_computation.2 | async-start | bytes 98304 | tf_op jit(solution)/shard_map/all_to_all | solution.py:320
  78.6 0.7 copy.22
  79.2 6.8 %all-to-all-done.2.refs_0_ = f32[16,3,2,128]{3,2,1,0:T(2,128)S(1)} async-done(((f32[16,3,2,128]{3,2,1,0:T(2,128)}), f32[16,3,2,128]{3,2,1,0:T(2,128)S(1)}, u32[]{:S(2)}, u32[]{:S(2)}) %all-to-all-start.2) | async-done | bytes 49184 | tf_op jit(solution)/shard_map/all_to_all | solution.py:320
  86.0 0.7 final.1
  (13 shorter events, 0.1 us)
Async XLA Ops:
  0.6 0.9 %copy-start = (bf16[2,1,128,256]{3,2,1,0:T(8,128)(2,1)S(1)}, bf16[2,1,128,256]{3,2,1,0:T(8,128)(2,1)}, u32[]{:S(2)}) copy-start(bf16[2,1,128,256]{3,2,1,0:T(8,128)(2,1)} %greens.1) | copy-start | bytes 393220
  2.4 14.0 %copy-start.5 = (s32[16,8]{0,1:T(8,128)S(1)}, s32[16,8]{0,1:T(8,128)}, u32[]{:S(2)}) copy-start(s32[16,8]{0,1:T(8,128)} %param.8) | copy-start | bytes 1540
  2.4 14.1 %copy-start.1 = (bf16[16,8,256]{2,1,0:T(8,128)(2,1)S(1)}, bf16[16,8,256]{2,1,0:T(8,128)(2,1)}, u32[]{:S(2)}) copy-start(bf16[16,8,256]{2,1,0:T(8,128)(2,1)} %refs_3_.1) | copy-start | bytes 196612
  2.4 31.3 %all-to-all-start = ((bf16[16,2,32,256]{3,2,1,0:T(8,128)(2,1)}), bf16[16,2,32,256]{3,2,1,0:T(8,128)(2,1)S(1)}, u32[]{:S(2)}, u32[]{:S(2)}) async-start(bf16[16,2,32,256]{3,2,1,0:T(8,128)(2,1)} %shard_map.85), calls=%async_computation | async-start | bytes 1048576 | tf_op jit(solution)/shard_map/all_to_all | solution.py:264
  16.4 0.7 copy-start.3
  16.4 0.7 copy-start.4
  36.0 22.9 %collective-permute-start = (bf16[32,16,256]{2,1,0:T(8,128)(2,1)S(1)}, bf16[32,16,256]{2,1,0:T(8,128)(2,1)S(1)}, u32[]{:S(2)}, u32[]{:S(2)}) collective-permute-start(bf16[32,16,256]{2,1,0:T(8,128)(2,1)S(1)} %get-tuple-element.25), channel_id=1, source_target_pairs={{0,16},{1,17},{2,18},{3,19},{4,20},{5,21},{6,22},{7,23},{16,32},{1... | collective-permute-start | bytes 786440 | tf_op jit(solution)/shard_map/ppermute | solution.py:285
  37.4 4.7 %collective-permute-start.1 = (bf16[8,8,256]{2,1,0:T(8,128)(2,1)S(1)}, bf16[8,8,256]{2,1,0:T(8,128)(2,1)S(1)}, u32[]{:S(2)}, u32[]{:S(2)}) collective-permute-start(bf16[8,8,256]{2,1,0:T(8,128)(2,1)S(1)} %dynamic-slice_bitcast_fusion.1), channel_id=1, source_target_pairs={{16,0},{17,1},{18,2},{19,3},{20,4},{21,5},{22,6},{23,7},{24,8},{25... | collective-permute-start | bytes 98312 | tf_op jit(solution)/shard_map/ppermute | solution.py:283
  43.2 27.1 %all-to-all-start.1 = ((bf16[48,4,128]{2,1,0:T(4,128)(2,1)}), bf16[48,4,128]{2,1,0:T(4,128)(2,1)S(1)}, u32[]{:S(2)}, u32[]{:S(2)}) async-start(bf16[48,4,128]{2,1,0:T(4,128)(2,1)} %overlap.1), calls=%async_computation.1 | async-start | bytes 98304 | tf_op jit(solution)/shard_map/all_to_all | solution.py:296
  59.0 0.7 copy-start.2
  71.0 15.1 %all-to-all-start.2 = ((f32[16,3,2,128]{3,2,1,0:T(2,128)}), f32[16,3,2,128]{3,2,1,0:T(2,128)S(1)}, u32[]{:S(2)}, u32[]{:S(2)}) async-start(f32[16,3,2,128]{3,2,1,0:T(2,128)} %combine.1), calls=%async_computation.2 | async-start | bytes 98304 | tf_op jit(solution)/shard_map/all_to_all | solution.py:320
